TPU v7x, 128 devices: a whole 4x4x4 slice. The times are simulated.
128 devices in a mesh: cent: 16 (over z, y), grp: 8 (over x, core).
Axes of the slice: x: 4, y: 4, z: 4, core: 2. Of those that a mesh axis runs over, the one named last changes fastest.
Arguments:
- queries: bfloat16 [256, 32, 128], P('grp'), may hold values from -6 to 6
- centroids: bfloat16 [524288, 128], P('cent'), may hold values from -0.5 to 0.5
- candidates: int32 [8, 16, 2, 64], P('grp', 'cent'), may hold values from 0 to 65535, as said below
- token_codes: int32 [65536, 128], P(('cent', 'grp')), may hold values from 0 to 32767
- resid_words: int32 [65536, 32, 128], P(('cent', 'grp')), may hold values from 0 to 255
- lengths: int32 [65536], P(('cent', 'grp')), may hold values from 1 to 128
- levels: float32 [4, 128], replicated, may hold values from -0.3125 to 0.3125
Outputs:
- token_best: float32 [256, 32], P('grp')
- passage_scores: float32 [8, 16, 2, 64], P('grp', 'cent')
Inputs may be any that keep to these rules, and one draw needn't show every extreme that they name: `candidates`: the entries of one [g, c] block are all different and name at most 2 passages of any one owner block (passages owner * 512 to owner * 512 + 511); one owner block gets exactly 2 from every [g, c] block.
All inputs are finite; a program needn't handle non-finite values.
Results may differ from a plain program's by a relative error of at most 0.0003.
Values may be sent and summed in bfloat16 or wider, within the bound.
A program may use at most 128 MiB of HBM per device.

v0:
```python
import functools

import jax
import jax.numpy as jnp
from jax import lax
from jax.experimental import pallas as pl
from jax.experimental.pallas import tpu as pltpu
from jax.sharding import PartitionSpec as P

MESH = pl.DeviceIdType.MESH
ANY = pl.BlockSpec(memory_space=pl.ANY)
VMEM = pl.BlockSpec(memory_space=pltpu.VMEM)
SMEM = pl.BlockSpec(memory_space=pltpu.SMEM)
EMPTY = 1 << 20
MASKED = -1000000000.0
UNITS = 8
BATCH = 16
PIECE = 1024
OPENING = 16


def greet(axis_peers):
    barrier = pltpu.get_barrier_semaphore()
    total = 0
    for axis, me, size in axis_peers:
        for d in range(1, size):
            pl.semaphore_signal(
                barrier, inc=1, device_id={axis: lax.rem(me + d, size)}, device_id_type=MESH
            )
            total += 1
    pl.semaphore_wait(barrier, total)


def push(src, dst, send, recv, axis, peer):
    return pltpu.make_async_remote_copy(
        src_ref=src,
        dst_ref=dst,
        send_sem=send,
        recv_sem=recv,
        device_id={axis: peer},
        device_id_type=MESH,
    )


def search_kernel(
    cents, groups, pass_dev, block, head, cand_count,
    q_ref, cand_ref, codes_ref, cent_hbm, words_hbm,
    table_ref, tail_ref, words_ref, qall_ref, qt_ref, acc_ref, picks_ref, ends_ref, entry_ref,
    head_buf, row_buf, all_buf, rows, csem, wsem, own_sem, s1, r1, s2, r2, sq, rq,
):
    me_c, me_g = lax.axis_index("cent"), lax.axis_index("grp")
    partner = me_g + 1 - 2 * lax.rem(me_g, 2)
    ahead, behind = lax.rem(me_g + 2, groups), lax.rem(me_g + groups - 2, groups)
    across = lax.rem(me_g + 4, groups)
    steps = head // block
    tiles, width = qt_ref.shape[0], qt_ref.shape[2]
    half = q_ref.shape[0] // 2

    def fetch(b):
        src = cent_hbm.at[pl.ds(pl.multiple_of(b * block, block), block)]
        return pltpu.make_async_copy(
            src, head_buf.at[pl.ds(pl.multiple_of(b * block, block), block)], csem.at[0, b]
        )

    def fetch_tail(b):
        src = cent_hbm.at[pl.ds(pl.multiple_of(head + b * block, block), block)]
        return pltpu.make_async_copy(
            src, tail_ref.at[pl.ds(pl.multiple_of(b * block, block), block)], csem.at[1, b]
        )

    for b in range(steps):
        fetch(b).start()
        fetch_tail(b).start()
    words_copy = pltpu.make_async_copy(words_hbm, words_ref, wsem)
    words_copy.start()
    own = pltpu.make_async_copy(q_ref, qall_ref.at[me_g], own_sem)
    own.start()
    row_buf[me_c] = jnp.concatenate([cand_ref[0:1, :], cand_ref[1:2, :]], axis=1)
    for t in range(tiles):
        qt_ref[t] = q_ref[t * width : (t + 1) * width, :].T
    acc_ref[...] = jnp.full(acc_ref.shape, -jnp.inf, jnp.float32)
    by_token = codes_ref[...].T
    for part in range(codes_ref.shape[1] // 32):
        span = slice(part * pass_dev, (part + 1) * pass_dev)
        picks_ref[:, span] = by_token[part * 32 : (part + 1) * 32, :]
    greet((("cent", me_c, cents), ("grp", me_g, groups)))

    gather_rows = [
        push(row_buf.at[me_c], row_buf.at[me_c], s1.at[d], r1.at[d], "cent", lax.rem(me_c + d, cents))
        for d in range(1, cents)
    ]
    gather_groups = [
        push(row_buf, all_buf.at[me_g], s2.at[d], r2.at[d], "grp", lax.rem(me_g + d, groups))
        for d in range(1, groups)
    ]

    def hand(k, block_of, peer, start=0, size=2 * half):
        held = qall_ref.at[block_of, pl.ds(start, size)]
        return push(held, held, sq.at[k], rq.at[k], "grp", peer)

    to_ahead = push(q_ref, qall_ref.at[me_g], sq.at[0], rq.at[0], "grp", ahead)
    to_behind = push(q_ref, qall_ref.at[me_g], sq.at[1], rq.at[1], "grp", behind)
    to_partner = push(q_ref, qall_ref.at[me_g], sq.at[2], rq.at[2], "grp", partner)
    relay_ahead = hand(3, behind, ahead, 0, half)
    relay_behind = hand(4, ahead, behind, half, half)
    share_behind = hand(5, behind, partner)
    share_ahead = hand(6, ahead, partner)
    share_low = hand(7, across, partner, 0, half)
    share_high = hand(8, across, partner, half, half)

    for copy in gather_rows:
        copy.start()
    to_ahead.start()
    to_behind.start()
    to_partner.start()

    def step(b, _):
        fetch(b).wait()
        fetch_tail(b).wait()

        @pl.when(b == min(2, steps - 1))
        def _():
            for copy in gather_rows:
                copy.wait_recv()
            for copy in gather_groups:
                copy.start()

        @pl.when(b == min(3, steps - 1))
        def _():
            to_ahead.wait_recv()
            relay_ahead.start()
            share_behind.start()
            to_behind.wait_recv()
            relay_behind.start()
            share_ahead.start()

        here = pl.ds(pl.multiple_of(b * block, block), block)
        there = pl.ds(pl.multiple_of(head + b * block, block), block)
        table_ref[here, :] = head_buf[here, :].astype(jnp.float32)
        table_ref[there, :] = tail_ref[here, :].astype(jnp.float32)
        for t in range(tiles):
            scores = jnp.dot(head_buf[here, :], qt_ref[t], preferred_element_type=jnp.float32)
            top = jnp.max(scores.reshape(block // 8, 8, width), axis=0)
            acc_ref[t] = jnp.maximum(acc_ref[t], top)
        return 0

    lax.fori_loop(0, steps, step, 0)

    relay_ahead.wait_recv()
    share_low.start()
    relay_behind.wait_recv()
    share_high.start()
    for copy in gather_groups:
        copy.wait_recv()
    all_buf[me_g] = row_buf[...]
    for g in range(groups):
        for c in range(cents):
            rows[pl.ds(g * cents + c, 1), :] = all_buf[g, c]
    found = rows[...]
    lane = lax.broadcasted_iota(jnp.int32, found.shape, 1)
    mine = jnp.right_shift(found, pass_dev.bit_length() - 1) == me_c * groups + me_g
    packed = (lane * pass_dev + jnp.bitwise_and(found, pass_dev - 1)).astype(jnp.float32)
    first = jnp.min(jnp.where(mine, packed, float(EMPTY)), axis=1, keepdims=True)
    last = jnp.max(jnp.where(mine, packed, -1.0), axis=1, keepdims=True)
    ends = jnp.where(lane == 0, first, jnp.where(lane == 1, last, 0.0))
    ends_ref[...] = ends
    turned = ends.T[0:8, :].astype(jnp.int32)
    source = lax.broadcasted_iota(jnp.int32, turned.shape, 1)
    slot = lax.broadcasted_iota(jnp.int32, turned.shape, 0)
    other = jnp.where(slot == 1, jnp.broadcast_to(turned[0:1, :], turned.shape), -1)
    there = (turned < EMPTY) & (turned > other)
    query = 2 * source + jnp.right_shift(turned, (pass_dev * cand_count).bit_length() - 1)
    entry = jnp.bitwise_and(turned, pass_dev - 1) + pass_dev * (
        query + 2 * cents * groups * (slot * cents * groups + source)
    )
    entry_ref[...] = jnp.where(there, entry, -1)

    own.wait()
    words_copy.wait()
    for copy in gather_rows + gather_groups:
        copy.wait_send()
    for copy in (to_ahead, to_behind, relay_ahead, relay_behind):
        copy.wait_send()
    for copy in (to_partner, share_behind, share_ahead, share_low, share_high):
        copy.wait()


def passage_kernel(
    cents, groups, pass_dev, plen, qtok, opening,
    entries, len_ref, ends_ref, lev_ref, picks_ref, table, tail, words, q_ref, qt_ref, acc_in,
    out_ref, best_ref,
    items, embeds, totals, acc, csem, *picks,
):
    srcs = groups * cents
    tiles = qt_ref.shape[0]
    rows_of_piece = PIECE
    pieces = tail.shape[0] // rows_of_piece * tiles
    loads = [
        pltpu.make_async_copy(picks_ref.at[r], picks[r], csem.at[r]) for r in range(len(picks))
    ]
    for copy in loads:
        copy.start()
    acc[...] = acc_in[...]

    def piece(m):
        t = lax.rem(m, tiles)
        start = pl.multiple_of(m // tiles * rows_of_piece, rows_of_piece)
        scores = jnp.dot(
            tail[pl.ds(start, rows_of_piece), :], qt_ref[t], preferred_element_type=jnp.float32
        )
        top = jnp.max(scores.reshape(rows_of_piece // 8, 8, scores.shape[1]), axis=0)
        acc[t] = jnp.maximum(acc[t], top)

    def collect(src, count):
        for slot in range(2):
            entry = entries[slot, src]
            items[count] = entry
            count = count + jnp.where(entry >= 0, 1, 0)
        return count

    def open_step(m, count):
        piece(m)
        for k in range(srcs // opening):
            count = collect(m * (srcs // opening) + k, count)
        return count

    count = lax.fori_loop(0, opening, open_step, jnp.int32(0))
    for pad in range(BATCH):
        items[count + pad] = 2 * srcs * (2 * srcs) * pass_dev
    totals[...] = jnp.zeros(totals.shape, jnp.float32)
    for copy in loads:
        copy.wait()

    sub = lax.broadcasted_iota(jnp.int32, (8, 128), 0)
    level = [jnp.broadcast_to(lev_ref[k : k + 1, :], (8, 128)) for k in range(4)]

    def embed(passage, part):
        word = words[passage, pl.ds(pl.multiple_of(part * 8, 8), 8), :]
        at = part * pass_dev + passage
        tiles = []
        for j in range(4):
            rows = None
            for s in range(8):
                row = table[pl.ds(picks[4 * s + j][at], 1), :]
                row = jnp.broadcast_to(row, (8, 128))
                rows = row if rows is None else jnp.where(sub == s, row, rows)
            low = jnp.bitwise_and(word, 1 << (2 * j)) != 0
            high = jnp.bitwise_and(word, 2 << (2 * j)) != 0
            residual = jnp.where(
                high, jnp.where(low, level[3], level[2]), jnp.where(low, level[1], level[0])
            )
            dense = rows + residual
            squares = jnp.sum(dense * dense, axis=1, keepdims=True)
            tiles.append(dense * lax.rsqrt(squares + 1e-06))
        return jnp.concatenate(tiles, axis=0).astype(jnp.bfloat16)

    def embed_units(item, part):
        done = []
        for _ in range(UNITS):
            passage = jnp.bitwise_and(items[item], pass_dev - 1)
            done.append((item, part, embed(passage, part)))
            ends = (part + 1) * 32 >= len_ref[passage]
            inside = item < count
            item, part = (
                jnp.where(inside & ends, item + 1, item),
                jnp.where(inside, jnp.where(ends, 0, part + 1), part),
            )
        for at, block, value in done:
            embeds[at, pl.ds(pl.multiple_of(block * 32, 32), 32), :] = value
        return item, part

    def both_step(state):
        item, part, m = state
        piece(m)
        item, part = embed_units(item, part)
        return item, part, m + 1

    def embed_step(state):
        return embed_units(*state)

    def piece_step(m, _):
        piece(m)
        return 0

    item, part, m = lax.while_loop(
        lambda s: (s[0] < count) & (s[2] < pieces),
        both_step,
        (jnp.int32(0), jnp.int32(0), jnp.int32(opening)),
    )
    lax.while_loop(lambda s: s[0] < count, embed_step, (item, part))
    lax.fori_loop(m, pieces, piece_step, 0)
    for t in range(tiles):
        width = acc.shape[2]
        best_ref[:, t * width : (t + 1) * width] = jnp.max(acc[t], axis=0, keepdims=True)

    sub_q = lax.broadcasted_iota(jnp.int32, (8, qtok), 0)

    def score_step(batch, _):
        for k in range(BATCH):
            i = batch * BATCH + k
            entry = items[i]
            query = jnp.bitwise_and(jnp.right_shift(entry, pass_dev.bit_length() - 1), 2 * srcs - 1)
            row = jnp.right_shift(entry, (2 * srcs * pass_dev).bit_length() - 1)
            length = len_ref[jnp.bitwise_and(entry, pass_dev - 1)]
            scores = lax.dot_general(
                embeds[i], q_ref[query], (((1,), (1,)), ((), ())), preferred_element_type=jnp.float32
            )
            top = None
            for part in range(plen // 32):
                for j in range(4):
                    at = part * 32 + j * 8
                    inside = 4 * sub_q + (part * 32 + j) < length
                    tile = jnp.where(inside, scores[at : at + 8], MASKED)
                    top = tile if top is None else jnp.maximum(top, tile)
            totals[pl.ds(row, 1), 0:qtok] = jnp.max(top, axis=0, keepdims=True)
        return 0

    lax.fori_loop(0, pl.cdiv(count, BATCH), score_step, 0)

    value = jnp.sum(totals[0 : 2 * srcs, :], axis=1, keepdims=True) * (1.0 / qtok)
    ends = ends_ref[...]
    lane = lax.broadcasted_iota(jnp.int32, (srcs, srcs), 1)
    place = jnp.right_shift(ends.astype(jnp.int32), pass_dev.bit_length() - 1)
    low, high = place[:, 0:1], place[:, 1:2]
    second = ends[:, 1:2] > ends[:, 0:1]
    out_ref[...] = jnp.where(lane == low, value[0:srcs], 0.0) + jnp.where(
        (lane == high) & second, value[srcs : 2 * srcs], 0.0
    )


def return_kernel(
    cents, groups,
    best_ref, part_ref,
    token_ref, score_ref,
    best_buf, part_buf, sum_buf, row_buf, sb, rb, s1, r1, s2, r2,
):
    me_c, me_g = lax.axis_index("cent"), lax.axis_index("grp")
    greet((("cent", me_c, cents), ("grp", me_g, groups)))

    def rows_of(g):
        return part_ref.at[pl.ds(pl.multiple_of(g * cents, cents), cents)]

    blocks, tops, lines = [], [], []
    for d in range(1, groups):
        peer = lax.rem(me_g + d, groups)
        blocks.append(push(rows_of(peer), part_buf.at[me_g], s1.at[d], r1.at[d], "grp", peer))
    for d in range(1, cents):
        peer = lax.rem(me_c + d, cents)
        tops.append(push(best_ref, best_buf.at[me_c], sb.at[d], rb.at[d], "cent", peer))
        lines.append(push(sum_buf.at[peer], row_buf.at[me_c], s2.at[d], r2.at[d], "cent", peer))
    for copy in blocks:
        copy.start()
    for copy in tops:
        copy.start()
    part_buf[me_g] = part_ref[pl.ds(pl.multiple_of(me_g * cents, cents), cents), :]
    best_buf[me_c] = best_ref[...]
    for copy in blocks:
        copy.wait_recv()
    total = part_buf[0]
    for g in range(1, groups):
        total = total + part_buf[g]
    for c in range(cents):
        sum_buf[c] = total[c : c + 1, :]
    row_buf[me_c] = sum_buf[me_c]
    for copy in lines:
        copy.start()

    for copy in tops:
        copy.wait_recv()
    top = best_buf[0]
    for c in range(1, cents):
        top = jnp.maximum(top, best_buf[c])
    width = token_ref.shape[1]
    for r in range(token_ref.shape[0]):
        token_ref[r : r + 1, :] = top[:, r * width : (r + 1) * width]

    for copy in lines:
        copy.wait_recv()
    line = row_buf[0]
    for c in range(1, cents):
        line = line + row_buf[c]
    half = score_ref.shape[1]
    score_ref[0:1, :] = line[:, 0:half]
    score_ref[1:2, :] = line[:, half : 2 * half]
    for copy in blocks + tops + lines:
        copy.wait_send()


def shards(queries, centroids, candidates, token_codes, resid_words, lengths, levels):
    query_rows, qtok, width = queries.shape
    cent_dev = centroids.shape[0]
    pass_dev, plen = token_codes.shape
    packed = resid_words.shape[1]
    per_device, cand_count = candidates.shape[2:]
    cents, groups = lax.axis_size("cent"), lax.axis_size("grp")
    srcs = cents * groups
    tokens = query_rows * qtok
    block, head = 4096, cent_dev // 2
    tiles = tokens // 256
    mib = 1 << 20
    dma = pltpu.SemaphoreType.DMA
    f32, i32, bf16 = jnp.float32, jnp.int32, jnp.bfloat16
    sds = jax.ShapeDtypeStruct
    hbm = functools.partial(pltpu.with_memory_space_constraint, memory_space=pltpu.HBM)

    table, tail, words, qall, qt, acc, picks, ends, entries = pl.pallas_call(
        functools.partial(search_kernel, cents, groups, pass_dev, block, head, cand_count),
        out_shape=(
            sds((cent_dev, width), f32),
            sds((cent_dev - head, width), bf16),
            sds((pass_dev, packed, width), i32),
            sds((groups, tokens, width), bf16),
            sds((tiles, width, 256), bf16),
            sds((tiles, 8, 256), f32),
            sds((32, plen // 32 * pass_dev), i32),
            sds((srcs, srcs), f32),
            sds((8, srcs), i32),
        ),
        in_specs=[VMEM, VMEM, VMEM, ANY, ANY],
        out_specs=(VMEM,) * 9,
        scratch_shapes=[
            pltpu.VMEM((head, width), bf16),
            pltpu.VMEM((cents, 1, srcs), i32),
            pltpu.VMEM((groups, cents, 1, srcs), i32),
            pltpu.VMEM((srcs, srcs), i32),
            dma((2, head // block)),
            dma,
            dma,
            dma((cents,)),
            dma((cents,)),
            dma((groups,)),
            dma((groups,)),
            dma((9,)),
            dma((9,)),
        ],
        compiler_params=pltpu.CompilerParams(
            collective_id=0, has_side_effects=True, vmem_limit_bytes=8 * mib
        ),
        name="search",
    )(
        queries.reshape(tokens, width),
        candidates.reshape(per_device, cand_count),
        token_codes,
        hbm(centroids),
        hbm(resid_words),
    )

    slots = 2 * srcs
    parts, best = pl.pallas_call(
        functools.partial(passage_kernel, cents, groups, pass_dev, plen, qtok, OPENING),
        out_shape=(sds((srcs, srcs), f32), sds((1, tokens), f32)),
        in_specs=[SMEM, SMEM, VMEM, VMEM, ANY, VMEM, VMEM, VMEM, VMEM, VMEM, VMEM],
        out_specs=(VMEM, VMEM),
        scratch_shapes=[
            pltpu.SMEM((slots + BATCH + 1,), i32),
            pltpu.VMEM((slots + BATCH, plen, width), bf16),
            pltpu.VMEM((slots + 8, 128), f32),
            pltpu.VMEM((tiles, 8, 256), f32),
            dma((32,)),
            *[pltpu.SMEM((plen // 32 * pass_dev,), i32) for _ in range(32)],
        ],
        compiler_params=pltpu.CompilerParams(vmem_limit_bytes=14 * mib),
        name="passages",
    )(
        entries,
        lengths,
        ends,
        levels,
        picks,
        table,
        tail,
        words,
        qall.reshape(groups * query_rows, qtok, width),
        qt,
        acc,
    )

    token_best, scores = pl.pallas_call(
        functools.partial(return_kernel, cents, groups),
        out_shape=(sds((query_rows, qtok), f32), sds((per_device, cand_count), f32)),
        in_specs=[VMEM, VMEM],
        out_specs=(VMEM, VMEM),
        scratch_shapes=[
            pltpu.VMEM((cents, 1, tokens), f32),
            pltpu.VMEM((groups, cents, srcs), f32),
            pltpu.VMEM((cents, 1, srcs), f32),
            pltpu.VMEM((cents, 1, srcs), f32),
            dma((cents,)),
            dma((cents,)),
            dma((groups,)),
            dma((groups,)),
            dma((cents,)),
            dma((cents,)),
        ],
        compiler_params=pltpu.CompilerParams(
            collective_id=1, has_side_effects=True, vmem_limit_bytes=4 * mib
        ),
        name="returns",
    )(best, parts)
    return token_best, scores.reshape(1, 1, per_device, cand_count)


def solution(mesh):
    placed = (
        P("grp", None, None),
        P("cent", None),
        P("grp", "cent", None, None),
        P(("cent", "grp"), None),
        P(("cent", "grp"), None, None),
        P(("cent", "grp")),
        P(),
    )
    return jax.shard_map(
        shards,
        mesh=mesh,
        in_specs=placed,
        out_specs=(P("grp", None), P("grp", "cent", None, None)),
        check_vma=False,
    )
```

profile of v0, /device:TPU:0, one launch (start us, length us, event | category | flops | bytes accessed | tf_op | source)
XLA Modules:
  0.0 75.1 jit_solution(712447897580824419)
XLA Ops:
  0.6 0.0 copy-start
  0.6 0.9 %copy-done = bf16[32,32,128]{2,1,0:T(8,128)(2,1)S(1)} copy-done((bf16[32,32,128]{2,1,0:T(8,128)(2,1)S(1)}, bf16[32,32,128]{2,1,0:T(8,128)(2,1)}, u32[]{:S(2)}) %copy-start) | copy-done | bytes 262168
  1.6 0.0 copy-start.1
  1.6 0.9 %copy-done.1 = s32[512,128]{1,0:T(8,128)S(1)} copy-done((s32[512,128]{1,0:T(8,128)S(1)}, s32[512,128]{1,0:T(8,128)}, u32[]{:S(2)}) %copy-start.1) | copy-done | bytes 262168
  2.5 0.0 copy-start.4
  2.5 0.7 copy-done.4
  3.2 0.0 copy-start.2
  3.2 0.0 copy-start.3
  3.2 22.8 %search.1 = (f32[32768,128]{1,0:T(8,128)S(1)}, bf16[16384,128]{1,0:T(8,128)(2,1)S(1)}, s32[512,32,128]{2,1,0:T(8,128)S(1)}, bf16[8,1024,128]{2,1,0:T(8,128)(2,1)...) custom-call(bf16[1024,128]{1,0:T(8,128)(2,1)S(1)} %bitcast.5, ...), custom_call_target="tpu_custom_call" | custom-call | tf_op jit(solution)/shard_map/search/pallas_call | solution.py:406
  26.0 0.0 copy-done.2
  26.0 0.0 copy-done.3
  26.0 30.1 %passages.1 = (f32[128,128]{1,0:T(8,128)S(1)}, f32[1,1024]{1,0:T(1,128)S(1)}) custom-call(s32[8,128]{1,0:T(8,128)S(1)} %get-tuple-element.15.entries, s32[512]{0:T(512)S(1)} %copy-done.2, f32[128,128]{1,0:T(8,128)S(1)} %get-tuple-element.16.ends_ref, f32[4,128]{1,0:T(4,128)S(1)} %copy-done.3, s32[32,2048]{1,0:T(8,128)S(1)} %get-tuple-element.17.picks_ref, ...), custom_call_target="tpu_custom_call" | custom-call | tf_op jit(solution)/shard_map/passages/pallas_call | solution.py:449
  56.1 17.8 %returns.1 = (f32[32,32]{1,0:T(8,128)S(1)}, f32[2,64]{1,0:T(2,128)S(1)}) custom-call(f32[1,1024]{1,0:T(1,128)S(1)} %get-tuple-element.24.best_ref, f32[128,128]{1,0:T(8,128)S(1)} %get-tuple-element.25.part_ref), custom_call_target="tpu_custom_call" | custom-call | tf_op jit(solution)/shard_map/returns/pallas_call | solution.py:478
  73.9 0.6 copy.11
  74.5 0.6 copy.12
Async XLA Ops:
  0.6 1.0 %copy-start = (bf16[32,32,128]{2,1,0:T(8,128)(2,1)S(1)}, bf16[32,32,128]{2,1,0:T(8,128)(2,1)}, u32[]{:S(2)}) copy-start(bf16[32,32,128]{2,1,0:T(8,128)(2,1)} %param.7) | copy-start | bytes 786436
  1.6 0.9 %copy-start.1 = (s32[512,128]{1,0:T(8,128)S(1)}, s32[512,128]{1,0:T(8,128)}, u32[]{:S(2)}) copy-start(s32[512,128]{1,0:T(8,128)} %codes_ref.1) | copy-start | bytes 786436
  2.5 0.7 copy-start.4
  3.2 22.8 %copy-start.2 = (s32[512]{0:T(512)S(1)}, s32[512]{0:T(512)}, u32[]{:S(2)}) copy-start(s32[512]{0:T(512)} %len_ref.1) | copy-start | bytes 6148
  3.2 22.8 %copy-start.3 = (f32[4,128]{1,0:T(4,128)S(1)}, f32[4,128]{1,0:T(4,128)}, u32[]{:S(2)}) copy-start(f32[4,128]{1,0:T(4,128)} %lev_ref.1) | copy-start | bytes 6148
where the time goes:
time: 75.5 us; the launch traced here: 75.1 us
  Pallas kernels  70.6 us (94%)
  local copies, waits for them, and re-layouts  3.75 us (5%)
    pallas_call x1, Pallas kernels, shards(): pl.pallas_call(functools.partial(passage_kernel, cents, groups, pass_dev,...  30.1 us
    pallas_call x1, Pallas kernels, shards(): pl.pallas_call(functools.partial(search_kernel, cents, groups, pass_dev,...  22.8 us
    pallas_call x1, Pallas kernels, shards(): pl.pallas_call(functools.partial(return_kernel, cents, groups), out_shape...  17.8 us
    unnamed x12, local copies, waits for them, and re-layouts  3.75 us

commit v1 on v0

--- a/solution.py
+++ b/solution.py
@@ -44,45 +44,45 @@
 
 def search_kernel(
     cents, groups, pass_dev, block, head, cand_count,
-    q_ref, cand_ref, codes_ref, cent_hbm, words_hbm,
+    q_hbm, cand_hbm, codes_hbm, cent_hbm, words_hbm,
     table_ref, tail_ref, words_ref, qall_ref, qt_ref, acc_ref, picks_ref, ends_ref, entry_ref,
-    head_buf, row_buf, all_buf, rows, csem, wsem, own_sem, s1, r1, s2, r2, sq, rq,
+    cand_ref, codes_ref, head_buf, row_buf, all_buf, rows, csem, tsem, wsem, own_sem, cand_sem, codes_sem, s1, r1, s2, r2, sq, rq,
 ):
     me_c, me_g = lax.axis_index("cent"), lax.axis_index("grp")
     partner = me_g + 1 - 2 * lax.rem(me_g, 2)
     ahead, behind = lax.rem(me_g + 2, groups), lax.rem(me_g + groups - 2, groups)
     across = lax.rem(me_g + 4, groups)
     steps = head // block
+    later = tail_ref.shape[0] // block
     tiles, width = qt_ref.shape[0], qt_ref.shape[2]
-    half = q_ref.shape[0] // 2
-
-    def fetch(b):
-        src = cent_hbm.at[pl.ds(pl.multiple_of(b * block, block), block)]
-        return pltpu.make_async_copy(
-            src, head_buf.at[pl.ds(pl.multiple_of(b * block, block), block)], csem.at[0, b]
+    half = q_hbm.shape[0] // 2
+    mine_q = qall_ref.at[me_g]
+
+    cand_copy = pltpu.make_async_copy(cand_hbm, cand_ref, cand_sem)
+    cand_copy.start()
+    own = pltpu.make_async_copy(q_hbm, mine_q, own_sem)
+    own.start()
+    fetch = [
+        pltpu.make_async_copy(
+            cent_hbm.at[pl.ds(b * block, block)], head_buf.at[pl.ds(b * block, block)], csem.at[b]
         )
-
-    def fetch_tail(b):
-        src = cent_hbm.at[pl.ds(pl.multiple_of(head + b * block, block), block)]
-        return pltpu.make_async_copy(
-            src, tail_ref.at[pl.ds(pl.multiple_of(b * block, block), block)], csem.at[1, b]
+        for b in range(steps)
+    ]
+    fetch_tail = [
+        pltpu.make_async_copy(
+            cent_hbm.at[pl.ds(head + b * block, block)], tail_ref.at[pl.ds(b * block, block)], tsem.at[b]
         )
-
-    for b in range(steps):
-        fetch(b).start()
-        fetch_tail(b).start()
+        for b in range(later)
+    ]
+    fetch[0].start()
+    codes_copy = pltpu.make_async_copy(codes_hbm, codes_ref, codes_sem)
+    codes_copy.start()
+    for copy in fetch[1:] + fetch_tail:
+        copy.start()
     words_copy = pltpu.make_async_copy(words_hbm, words_ref, wsem)
     words_copy.start()
-    own = pltpu.make_async_copy(q_ref, qall_ref.at[me_g], own_sem)
-    own.start()
+    cand_copy.wait()
     row_buf[me_c] = jnp.concatenate([cand_ref[0:1, :], cand_ref[1:2, :]], axis=1)
-    for t in range(tiles):
-        qt_ref[t] = q_ref[t * width : (t + 1) * width, :].T
-    acc_ref[...] = jnp.full(acc_ref.shape, -jnp.inf, jnp.float32)
-    by_token = codes_ref[...].T
-    for part in range(codes_ref.shape[1] // 32):
-        span = slice(part * pass_dev, (part + 1) * pass_dev)
-        picks_ref[:, span] = by_token[part * 32 : (part + 1) * 32, :]
     greet((("cent", me_c, cents), ("grp", me_g, groups)))
 
     gather_rows = [
@@ -98,9 +98,9 @@
         held = qall_ref.at[block_of, pl.ds(start, size)]
         return push(held, held, sq.at[k], rq.at[k], "grp", peer)
 
-    to_ahead = push(q_ref, qall_ref.at[me_g], sq.at[0], rq.at[0], "grp", ahead)
-    to_behind = push(q_ref, qall_ref.at[me_g], sq.at[1], rq.at[1], "grp", behind)
-    to_partner = push(q_ref, qall_ref.at[me_g], sq.at[2], rq.at[2], "grp", partner)
+    to_ahead = push(mine_q, mine_q, sq.at[0], rq.at[0], "grp", ahead)
+    to_behind = push(mine_q, mine_q, sq.at[1], rq.at[1], "grp", behind)
+    to_partner = push(mine_q, mine_q, sq.at[2], rq.at[2], "grp", partner)
     relay_ahead = hand(3, behind, ahead, 0, half)
     relay_behind = hand(4, ahead, behind, half, half)
     share_behind = hand(5, behind, partner)
@@ -110,22 +110,32 @@
 
     for copy in gather_rows:
         copy.start()
+    own.wait()
     to_ahead.start()
     to_behind.start()
     to_partner.start()
 
+    for t in range(tiles):
+        qt_ref[t] = qall_ref[me_g, t * width : (t + 1) * width, :].T
+    acc_ref[...] = jnp.full(acc_ref.shape, -jnp.inf, jnp.float32)
+    codes_copy.wait()
+    by_token = codes_ref[...].T
+    for part in range(codes_ref.shape[1] // 32):
+        span = slice(part * pass_dev, (part + 1) * pass_dev)
+        picks_ref[:, span] = by_token[part * 32 : (part + 1) * 32, :]
+
     def step(b, _):
-        fetch(b).wait()
-        fetch_tail(b).wait()
-
-        @pl.when(b == min(2, steps - 1))
+        here = pl.ds(pl.multiple_of(b * block, block), block)
+        pltpu.make_async_copy(cent_hbm.at[here], head_buf.at[here], csem.at[b]).wait()
+
+        @pl.when(b == 1)
         def _():
             for copy in gather_rows:
                 copy.wait_recv()
             for copy in gather_groups:
                 copy.start()
 
-        @pl.when(b == min(3, steps - 1))
+        @pl.when(b == 2)
         def _():
             to_ahead.wait_recv()
             relay_ahead.start()
@@ -134,10 +144,7 @@
             relay_behind.start()
             share_ahead.start()
 
-        here = pl.ds(pl.multiple_of(b * block, block), block)
-        there = pl.ds(pl.multiple_of(head + b * block, block), block)
         table_ref[here, :] = head_buf[here, :].astype(jnp.float32)
-        table_ref[there, :] = tail_ref[here, :].astype(jnp.float32)
         for t in range(tiles):
             scores = jnp.dot(head_buf[here, :], qt_ref[t], preferred_element_type=jnp.float32)
             top = jnp.max(scores.reshape(block // 8, 8, width), axis=0)
@@ -145,6 +152,17 @@
         return 0
 
     lax.fori_loop(0, steps, step, 0)
+    for copy in fetch_tail:
+        copy.wait()
+    part_rows = 1024
+
+    def widen(r, _):
+        src = pl.ds(pl.multiple_of(r * part_rows, part_rows), part_rows)
+        dst = pl.ds(pl.multiple_of(head + r * part_rows, part_rows), part_rows)
+        table_ref[dst, :] = tail_ref[src, :].astype(jnp.float32)
+        return 0
+
+    lax.fori_loop(0, tail_ref.shape[0] // part_rows, widen, 0)
 
     relay_ahead.wait_recv()
     share_low.start()
@@ -175,7 +193,6 @@
     )
     entry_ref[...] = jnp.where(there, entry, -1)
 
-    own.wait()
     words_copy.wait()
     for copy in gather_rows + gather_groups:
         copy.wait_send()
@@ -189,7 +206,7 @@
     cents, groups, pass_dev, plen, qtok, opening,
     entries, len_ref, ends_ref, lev_ref, picks_ref, table, tail, words, q_ref, qt_ref, acc_in,
     out_ref, best_ref,
-    items, embeds, totals, acc, csem, *picks,
+    items, starts, units, embeds, totals, acc, spread, csem, *picks,
 ):
     srcs = groups * cents
     tiles = qt_ref.shape[0]
@@ -211,22 +228,35 @@
         top = jnp.max(scores.reshape(rows_of_piece // 8, 8, scores.shape[1]), axis=0)
         acc[t] = jnp.maximum(acc[t], top)
 
-    def collect(src, count):
+    def collect(src, state):
+        count, used = state
         for slot in range(2):
             entry = entries[slot, src]
+            passage = jnp.bitwise_and(entry, pass_dev - 1)
+            parts = jnp.right_shift(len_ref[passage] + 31, 5)
             items[count] = entry
-            count = count + jnp.where(entry >= 0, 1, 0)
-        return count
-
-    def open_step(m, count):
+            starts[count] = used
+            for part in range(plen // 32):
+                units[used + part] = passage + part * pass_dev
+            there = entry >= 0
+            count = count + jnp.where(there, 1, 0)
+            used = used + jnp.where(there, parts, 0)
+        return count, used
+
+    def open_step(m, state):
         piece(m)
         for k in range(srcs // opening):
-            count = collect(m * (srcs // opening) + k, count)
-        return count
-
-    count = lax.fori_loop(0, opening, open_step, jnp.int32(0))
+            state = collect(m * (srcs // opening) + k, state)
+        return state
+
+    for k in range(len(spread)):
+        spread[k][...] = jnp.zeros(spread[k].shape, spread[k].dtype)
+    count, used = lax.fori_loop(0, opening, open_step, (jnp.int32(0), jnp.int32(0)))
     for pad in range(BATCH):
         items[count + pad] = 2 * srcs * (2 * srcs) * pass_dev
+        starts[count + pad] = 0
+    for pad in range(UNITS):
+        units[used + pad] = 0
     totals[...] = jnp.zeros(totals.shape, jnp.float32)
     for copy in loads:
         copy.wait()
@@ -234,9 +264,10 @@
     sub = lax.broadcasted_iota(jnp.int32, (8, 128), 0)
     level = [jnp.broadcast_to(lev_ref[k : k + 1, :], (8, 128)) for k in range(4)]
 
-    def embed(passage, part):
+    def embed(at):
+        passage = jnp.bitwise_and(at, pass_dev - 1)
+        part = jnp.right_shift(at, pass_dev.bit_length() - 1)
         word = words[passage, pl.ds(pl.multiple_of(part * 8, 8), 8), :]
-        at = part * pass_dev + passage
         tiles = []
         for j in range(4):
             rows = None
@@ -254,65 +285,61 @@
             tiles.append(dense * lax.rsqrt(squares + 1e-06))
         return jnp.concatenate(tiles, axis=0).astype(jnp.bfloat16)
 
-    def embed_units(item, part):
-        done = []
-        for _ in range(UNITS):
-            passage = jnp.bitwise_and(items[item], pass_dev - 1)
-            done.append((item, part, embed(passage, part)))
-            ends = (part + 1) * 32 >= len_ref[passage]
-            inside = item < count
-            item, part = (
-                jnp.where(inside & ends, item + 1, item),
-                jnp.where(inside, jnp.where(ends, 0, part + 1), part),
-            )
-        for at, block, value in done:
-            embeds[at, pl.ds(pl.multiple_of(block * 32, 32), 32), :] = value
-        return item, part
-
-    def both_step(state):
-        item, part, m = state
-        piece(m)
-        item, part = embed_units(item, part)
-        return item, part, m + 1
-
-    def embed_step(state):
-        return embed_units(*state)
+    def embed_step(i, _):
+        values = [embed(units[i * UNITS + k]) for k in range(UNITS)]
+        for k, value in enumerate(values):
+            embeds[pl.ds(pl.multiple_of(i * (UNITS * 32) + k * 32, 32), 32), :] = value
+        return 0
 
     def piece_step(m, _):
         piece(m)
         return 0
 
-    item, part, m = lax.while_loop(
-        lambda s: (s[0] < count) & (s[2] < pieces),
-        both_step,
-        (jnp.int32(0), jnp.int32(0), jnp.int32(opening)),
-    )
-    lax.while_loop(lambda s: s[0] < count, embed_step, (item, part))
-    lax.fori_loop(m, pieces, piece_step, 0)
+    def both_step(i, _):
+        piece(opening + i)
+        return embed_step(i, 0)
+
+    turns = pl.cdiv(used, UNITS)
+    shared = jnp.minimum(turns, pieces - opening)
+    lax.fori_loop(0, shared, both_step, 0)
+    lax.fori_loop(shared, turns, embed_step, 0)
+    lax.fori_loop(opening + shared, pieces, piece_step, 0)
+    embeds[pl.ds(pl.multiple_of(turns * (UNITS * 32), 32), plen), :] = jnp.zeros(
+        (plen, embeds.shape[1]), embeds.dtype
+    )
     for t in range(tiles):
         width = acc.shape[2]
         best_ref[:, t * width : (t + 1) * width] = jnp.max(acc[t], axis=0, keepdims=True)
 
-    sub_q = lax.broadcasted_iota(jnp.int32, (8, qtok), 0)
+    lane_q = lax.broadcasted_iota(jnp.int32, (8, 128), 1)
+    four = 128 // qtok
 
     def score_step(batch, _):
-        for k in range(BATCH):
-            i = batch * BATCH + k
-            entry = items[i]
-            query = jnp.bitwise_and(jnp.right_shift(entry, pass_dev.bit_length() - 1), 2 * srcs - 1)
-            row = jnp.right_shift(entry, (2 * srcs * pass_dev).bit_length() - 1)
-            length = len_ref[jnp.bitwise_and(entry, pass_dev - 1)]
+        for k, wide in enumerate(spread):
+            limit, rows, held = None, [], []
+            for n in range(four):
+                i = batch * BATCH + k * four + n
+                entry = items[i]
+                query = jnp.bitwise_and(jnp.right_shift(entry, pass_dev.bit_length() - 1), 2 * srcs - 1)
+                rows.append(jnp.right_shift(entry, (2 * srcs * pass_dev).bit_length() - 1))
+                length = len_ref[jnp.bitwise_and(entry, pass_dev - 1)]
+                wide[n * qtok : (n + 1) * qtok, n * 128 : (n + 1) * 128] = q_ref[query]
+                limit = length if limit is None else jnp.where(lane_q >= n * qtok, length, limit)
+                held.append(embeds[pl.ds(pl.multiple_of(starts[i] * 32, 32), plen), :])
             scores = lax.dot_general(
-                embeds[i], q_ref[query], (((1,), (1,)), ((), ())), preferred_element_type=jnp.float32
+                jnp.concatenate(held, axis=1), wide[...], (((1,), (1,)), ((), ())), preferred_element_type=jnp.float32
             )
             top = None
             for part in range(plen // 32):
                 for j in range(4):
                     at = part * 32 + j * 8
-                    inside = 4 * sub_q + (part * 32 + j) < length
+                    inside = 4 * sub + (part * 32 + j) < limit
                     tile = jnp.where(inside, scores[at : at + 8], MASKED)
                     top = tile if top is None else jnp.maximum(top, tile)
-            totals[pl.ds(row, 1), 0:qtok] = jnp.max(top, axis=0, keepdims=True)
+            line = jnp.max(top, axis=0, keepdims=True)
+            for n in range(four):
+                own = (lane_q[0:1] >= n * qtok) & (lane_q[0:1] < (n + 1) * qtok)
+                totals[pl.ds(rows[n], 1), :] = jnp.where(own, line, 0.0)
         return 0
 
     lax.fori_loop(0, pl.cdiv(count, BATCH), score_step, 0)
@@ -395,7 +422,7 @@
     cents, groups = lax.axis_size("cent"), lax.axis_size("grp")
     srcs = cents * groups
     tokens = query_rows * qtok
-    block, head = 4096, cent_dev // 2
+    block, head = 4096, 3 * cent_dev // 8
     tiles = tokens // 256
     mib = 1 << 20
     dma = pltpu.SemaphoreType.DMA
@@ -416,14 +443,19 @@
             sds((srcs, srcs), f32),
             sds((8, srcs), i32),
         ),
-        in_specs=[VMEM, VMEM, VMEM, ANY, ANY],
+        in_specs=[ANY] * 5,
         out_specs=(VMEM,) * 9,
         scratch_shapes=[
+            pltpu.VMEM((per_device, cand_count), i32),
+            pltpu.VMEM((pass_dev, plen), i32),
             pltpu.VMEM((head, width), bf16),
             pltpu.VMEM((cents, 1, srcs), i32),
             pltpu.VMEM((groups, cents, 1, srcs), i32),
             pltpu.VMEM((srcs, srcs), i32),
-            dma((2, head // block)),
+            dma((head // block,)),
+            dma(((cent_dev - head) // block,)),
+            dma,
+            dma,
             dma,
             dma,
             dma((cents,)),
@@ -438,9 +470,9 @@
         ),
         name="search",
     )(
-        queries.reshape(tokens, width),
-        candidates.reshape(per_device, cand_count),
-        token_codes,
+        hbm(queries.reshape(tokens, width)),
+        hbm(candidates.reshape(per_device, cand_count)),
+        hbm(token_codes),
         hbm(centroids),
         hbm(resid_words),
     )
@@ -452,10 +484,13 @@
         in_specs=[SMEM, SMEM, VMEM, VMEM, ANY, VMEM, VMEM, VMEM, VMEM, VMEM, VMEM],
         out_specs=(VMEM, VMEM),
         scratch_shapes=[
-            pltpu.SMEM((slots + BATCH + 1,), i32),
-            pltpu.VMEM((slots + BATCH, plen, width), bf16),
+            pltpu.SMEM((slots + BATCH,), i32),
+            pltpu.SMEM((slots + BATCH,), i32),
+            pltpu.SMEM((slots * (plen // 32) + UNITS + 4,), i32),
+            pltpu.VMEM((slots * plen + UNITS * 32 + plen, width), bf16),
             pltpu.VMEM((slots + 8, 128), f32),
             pltpu.VMEM((tiles, 8, 256), f32),
+            [pltpu.VMEM((128, 128 // qtok * width), bf16) for _ in range(BATCH * qtok // 128)],
             dma((32,)),
             *[pltpu.SMEM((plen // 32 * pass_dev,), i32) for _ in range(32)],
         ],

time: 75.5 us -> 75.3 us (level)
  local copies, waits for them, and re-layouts: 3.75 us -> 1.18 us
  Pallas kernels: 70.6 us -> 73 us
    pallas_call x1, Pallas kernels: 30.1 us -> 34.9 us  [shards(): pl.pallas_call(functools.partial(passage_kernel, cents, groups, pass_dev,...]
    pallas_call x1, Pallas kernels: 17.8 us -> 14 us  [shards(): pl.pallas_call(functools.partial(return_kernel, cents, groups), out_shape...]
    unnamed x12 -> x6, local copies, waits for them, and re-layouts: 3.75 us -> 1.18 us
    pallas_call x1, Pallas kernels: 22.8 us -> 24.2 us  [shards(): pl.pallas_call(functools.partial(search_kernel, cents, groups, pass_dev,...]
where the time goes in v1:
time: 75.3 us; the launch traced here: 74.9 us
  Pallas kernels  73 us (97%)
  local copies, waits for them, and re-layouts  1.18 us (2%)
    pallas_call x1, Pallas kernels, shards(): pl.pallas_call(functools.partial(passage_kernel, cents, groups, pass_dev,...  34.9 us
    pallas_call x1, Pallas kernels, shards(): pl.pallas_call(functools.partial(search_kernel, cents, groups, pass_dev,...  24.2 us
    pallas_call x1, Pallas kernels, shards(): pl.pallas_call(functools.partial(return_kernel, cents, groups), out_shape...  14 us

profile of v1, /device:TPU:0, one launch (start us, length us, event | category | flops | bytes accessed | tf_op | source)
XLA Modules:
  0.0 74.9 jit_solution(18107397305796654324)
XLA Ops:
  0.6 0.0 copy-start
  0.6 0.0 copy-start.1
  0.7 24.2 %search.1 = (f32[32768,128]{1,0:T(8,128)S(1)}, bf16[20480,128]{1,0:T(8,128)(2,1)S(1)}, s32[512,32,128]{2,1,0:T(8,128)S(1)}, bf16[8,1024,128]{2,1,0:T(8,128)(2,1)...) custom-call(bf16[1024,128]{1,0:T(8,128)(2,1)} %bitcast.6, ...), custom_call_target="tpu_custom_call" | custom-call | tf_op jit(solution)/shard_map/search/pallas_call | solution.py:433
  24.8 0.0 copy-done
  24.8 0.0 copy-done.1
  24.8 34.9 %passages.1 = (f32[128,128]{1,0:T(8,128)S(1)}, f32[1,1024]{1,0:T(1,128)S(1)}) custom-call(s32[8,128]{1,0:T(8,128)S(1)} %get-tuple-element.15.entries, s32[512]{0:T(512)S(1)} %copy-done, f32[128,128]{1,0:T(8,128)S(1)} %get-tuple-element.16.ends_ref, f32[4,128]{1,0:T(4,128)S(1)} %copy-done.1, s32[32,2048]{1,0:T(8,128)S(1)} %get-tuple-element.17.picks_ref, ...), custom_call_target="tpu_custom_call" | custom-call | tf_op jit(solution)/shard_map/passages/pallas_call | solution.py:481
  59.7 14.0 %returns.1 = (f32[32,32]{1,0:T(8,128)S(1)}, f32[2,64]{1,0:T(2,128)S(1)}) custom-call(f32[1,1024]{1,0:T(1,128)S(1)} %get-tuple-element.24.best_ref, f32[128,128]{1,0:T(8,128)S(1)} %get-tuple-element.25.part_ref), custom_call_target="tpu_custom_call" | custom-call | tf_op jit(solution)/shard_map/returns/pallas_call | solution.py:513
  73.7 0.6 copy.11
  74.4 0.6 copy.12
Async XLA Ops:
  0.6 24.2 %copy-start = (s32[512]{0:T(512)S(1)}, s32[512]{0:T(512)}, u32[]{:S(2)}) copy-start(s32[512]{0:T(512)} %len_ref.1) | copy-start | bytes 6148
  0.6 24.2 %copy-start.1 = (f32[4,128]{1,0:T(4,128)S(1)}, f32[4,128]{1,0:T(4,128)}, u32[]{:S(2)}) copy-start(f32[4,128]{1,0:T(4,128)} %lev_ref.1) | copy-start | bytes 6148

commit v2 on v1

--- a/solution.py
+++ b/solution.py
@@ -14,7 +14,7 @@
 EMPTY = 1 << 20
 MASKED = -1000000000.0
 UNITS = 8
-BATCH = 16
+BATCH = 32
 PIECE = 1024
 OPENING = 16
 
@@ -94,26 +94,30 @@
         for d in range(1, groups)
     ]
 
-    def hand(k, block_of, peer, start=0, size=2 * half):
-        held = qall_ref.at[block_of, pl.ds(start, size)]
+    low, high = pl.ds(0, half), pl.ds(half, half)
+    lanes = iter(range(sq.shape[0]))
+
+    def hand(block_of, span, peer):
+        k = next(lanes)
+        held = qall_ref.at[block_of, span]
         return push(held, held, sq.at[k], rq.at[k], "grp", peer)
 
-    to_ahead = push(mine_q, mine_q, sq.at[0], rq.at[0], "grp", ahead)
-    to_behind = push(mine_q, mine_q, sq.at[1], rq.at[1], "grp", behind)
-    to_partner = push(mine_q, mine_q, sq.at[2], rq.at[2], "grp", partner)
-    relay_ahead = hand(3, behind, ahead, 0, half)
-    relay_behind = hand(4, ahead, behind, half, half)
-    share_behind = hand(5, behind, partner)
-    share_ahead = hand(6, ahead, partner)
-    share_low = hand(7, across, partner, 0, half)
-    share_high = hand(8, across, partner, half, half)
+    ahead_low, behind_high = hand(me_g, low, ahead), hand(me_g, high, behind)
+    ahead_high, behind_low = hand(me_g, high, ahead), hand(me_g, low, behind)
+    to_partner = hand(me_g, pl.ds(0, 2 * half), partner)
+    relay_ahead, relay_behind = hand(behind, low, ahead), hand(ahead, high, behind)
+    shares = [
+        hand(block_of, span, partner)
+        for block_of, span in (
+            (behind, low), (ahead, high), (behind, high), (ahead, low), (across, low), (across, high)
+        )
+    ]
 
     for copy in gather_rows:
         copy.start()
     own.wait()
-    to_ahead.start()
-    to_behind.start()
-    to_partner.start()
+    for copy in (ahead_low, behind_high, ahead_high, behind_low, to_partner):
+        copy.start()
 
     for t in range(tiles):
         qt_ref[t] = qall_ref[me_g, t * width : (t + 1) * width, :].T
@@ -128,21 +132,28 @@
         here = pl.ds(pl.multiple_of(b * block, block), block)
         pltpu.make_async_copy(cent_hbm.at[here], head_buf.at[here], csem.at[b]).wait()
 
-        @pl.when(b == 1)
+        @pl.when(b == 2)
         def _():
             for copy in gather_rows:
                 copy.wait_recv()
             for copy in gather_groups:
                 copy.start()
 
-        @pl.when(b == 2)
+        @pl.when(b == 3)
         def _():
-            to_ahead.wait_recv()
+            ahead_low.wait_recv()
             relay_ahead.start()
-            share_behind.start()
-            to_behind.wait_recv()
+            shares[0].start()
+            behind_high.wait_recv()
             relay_behind.start()
-            share_ahead.start()
+            shares[1].start()
+
+        @pl.when(b == 6)
+        def _():
+            ahead_high.wait_recv()
+            shares[2].start()
+            behind_low.wait_recv()
+            shares[3].start()
 
         table_ref[here, :] = head_buf[here, :].astype(jnp.float32)
         for t in range(tiles):
@@ -165,9 +176,9 @@
     lax.fori_loop(0, tail_ref.shape[0] // part_rows, widen, 0)
 
     relay_ahead.wait_recv()
-    share_low.start()
+    shares[4].start()
     relay_behind.wait_recv()
-    share_high.start()
+    shares[5].start()
     for copy in gather_groups:
         copy.wait_recv()
     all_buf[me_g] = row_buf[...]
@@ -196,9 +207,9 @@
     words_copy.wait()
     for copy in gather_rows + gather_groups:
         copy.wait_send()
-    for copy in (to_ahead, to_behind, relay_ahead, relay_behind):
+    for copy in (ahead_low, behind_high, ahead_high, behind_low, relay_ahead, relay_behind):
         copy.wait_send()
-    for copy in (to_partner, share_behind, share_ahead, share_low, share_high):
+    for copy in [to_partner] + shares:
         copy.wait()
 
 
@@ -206,7 +217,7 @@
     cents, groups, pass_dev, plen, qtok, opening,
     entries, len_ref, ends_ref, lev_ref, picks_ref, table, tail, words, q_ref, qt_ref, acc_in,
     out_ref, best_ref,
-    items, starts, units, embeds, totals, acc, spread, csem, *picks,
+    items, starts, units, seen, embeds, totals, acc, spread, csem, *picks,
 ):
     srcs = groups * cents
     tiles = qt_ref.shape[0]
@@ -230,17 +241,21 @@
 
     def collect(src, state):
         count, used = state
-        for slot in range(2):
-            entry = entries[slot, src]
-            passage = jnp.bitwise_and(entry, pass_dev - 1)
-            parts = jnp.right_shift(len_ref[passage] + 31, 5)
-            items[count] = entry
-            starts[count] = used
+        pair = [entries[slot * srcs + src] for slot in range(2)]
+        there = [entry >= 0 for entry in pair]
+        owned = [jnp.bitwise_and(entry, pass_dev - 1) for entry in pair]
+        marks = [jnp.where(ok, passage, pass_dev) for ok, passage in zip(there, owned)]
+        known = [seen[mark] for mark in marks]
+        sizes = [jnp.right_shift(len_ref[passage] + 31, 5) for passage in owned]
+        for n in range(2):
+            at = jnp.where(known[n] < 0, used, known[n])
+            items[count] = pair[n]
+            starts[count] = at
+            seen[marks[n]] = at
             for part in range(plen // 32):
-                units[used + part] = passage + part * pass_dev
-            there = entry >= 0
-            count = count + jnp.where(there, 1, 0)
-            used = used + jnp.where(there, parts, 0)
+                units[used + part] = owned[n] + part * pass_dev
+            count = count + jnp.where(there[n], 1, 0)
+            used = used + jnp.where(there[n] & (known[n] < 0), sizes[n], 0)
         return count, used
 
     def open_step(m, state):
@@ -251,6 +266,11 @@
 
     for k in range(len(spread)):
         spread[k][...] = jnp.zeros(spread[k].shape, spread[k].dtype)
+    def forget(k, _):
+        seen[k] = -1
+        return 0
+
+    lax.fori_loop(0, pass_dev, forget, 0, unroll=16)
     count, used = lax.fori_loop(0, opening, open_step, (jnp.int32(0), jnp.int32(0)))
     for pad in range(BATCH):
         items[count + pad] = 2 * srcs * (2 * srcs) * pass_dev
@@ -422,7 +442,7 @@
     cents, groups = lax.axis_size("cent"), lax.axis_size("grp")
     srcs = cents * groups
     tokens = query_rows * qtok
-    block, head = 4096, 3 * cent_dev // 8
+    block, head = 2048, cent_dev // 2
     tiles = tokens // 256
     mib = 1 << 20
     dma = pltpu.SemaphoreType.DMA
@@ -462,8 +482,8 @@
             dma((cents,)),
             dma((groups,)),
             dma((groups,)),
-            dma((9,)),
-            dma((9,)),
+            dma((13,)),
+            dma((13,)),
         ],
         compiler_params=pltpu.CompilerParams(
             collective_id=0, has_side_effects=True, vmem_limit_bytes=8 * mib
@@ -487,6 +507,7 @@
             pltpu.SMEM((slots + BATCH,), i32),
             pltpu.SMEM((slots + BATCH,), i32),
             pltpu.SMEM((slots * (plen // 32) + UNITS + 4,), i32),
+            pltpu.SMEM((pass_dev + 1,), i32),
             pltpu.VMEM((slots * plen + UNITS * 32 + plen, width), bf16),
             pltpu.VMEM((slots + 8, 128), f32),
             pltpu.VMEM((tiles, 8, 256), f32),
@@ -497,7 +518,7 @@
         compiler_params=pltpu.CompilerParams(vmem_limit_bytes=14 * mib),
         name="passages",
     )(
-        entries,
+        entries.reshape(8 * srcs),
         lengths,
         ends,
         levels,

time: 75.3 us -> 69.6 us (0.924)
  Pallas kernels: 73 us -> 67.3 us
    pallas_call x1, Pallas kernels: 34.9 us -> 25.4 us  [shards(): pl.pallas_call(functools.partial(passage_kernel, cents, groups, pass_dev,...]
    pallas_call x1, Pallas kernels: 24.2 us -> 26.1 us  [shards(): pl.pallas_call(functools.partial(search_kernel, cents, groups, pass_dev,...]
    pallas_call x1, Pallas kernels: 14 us -> 15.8 us  [shards(): pl.pallas_call(functools.partial(return_kernel, cents, groups), out_shape...]
where the time goes in v2:
time: 69.6 us; the launch traced here: 69.2 us
  Pallas kernels  67.3 us (97%)
  local copies, waits for them, and re-layouts  1.18 us (2%)
    pallas_call x1, Pallas kernels, shards(): pl.pallas_call(functools.partial(search_kernel, cents, groups, pass_dev,...  26.1 us
    pallas_call x1, Pallas kernels, shards(): pl.pallas_call(functools.partial(passage_kernel, cents, groups, pass_dev,...  25.4 us
    pallas_call x1, Pallas kernels, shards(): pl.pallas_call(functools.partial(return_kernel, cents, groups), out_shape...  15.8 us

profile of v2, /device:TPU:0, one launch (start us, length us, event | category | flops | bytes accessed | tf_op | source)
XLA Modules:
  0.0 69.2 jit_solution(9244209364012608412)
XLA Ops:
  0.6 0.0 copy-start
  0.6 0.0 copy-start.1
  0.7 26.1 %search.1 = (f32[32768,128]{1,0:T(8,128)S(1)}, bf16[16384,128]{1,0:T(8,128)(2,1)S(1)}, s32[512,32,128]{2,1,0:T(8,128)S(1)}, bf16[8,1024,128]{2,1,0:T(8,128)(2,1)...) custom-call(bf16[1024,128]{1,0:T(8,128)(2,1)} %bitcast.8, ...), custom_call_target="tpu_custom_call" | custom-call | tf_op jit(solution)/shard_map/search/pallas_call | solution.py:453
  26.8 0.0 copy-done
  26.8 0.0 copy-done.1
  26.8 25.4 %passages.1 = (f32[128,128]{1,0:T(8,128)S(1)}, f32[1,1024]{1,0:T(1,128)S(1)}) custom-call(s32[1024]{0:T(1024)S(1)} %bitcast.6, s32[512]{0:T(512)S(1)} %copy-done, f32[128,128]{1,0:T(8,128)S(1)} %get-tuple-element.16.ends_ref, f32[4,128]{1,0:T(4,128)S(1)} %copy-done.1, s32[32,2048]{1,0:T(8,128)S(1)} %get-tuple-element.17.picks_ref, ...), custom_call_target="tpu_custom_call" | custom-call | tf_op jit(solution)/shard_map/passages/pallas_call | solution.py:501
  52.2 15.8 %returns.1 = (f32[32,32]{1,0:T(8,128)S(1)}, f32[2,64]{1,0:T(2,128)S(1)}) custom-call(f32[1,1024]{1,0:T(1,128)S(1)} %get-tuple-element.24.best_ref, f32[128,128]{1,0:T(8,128)S(1)} %get-tuple-element.25.part_ref), custom_call_target="tpu_custom_call" | custom-call | tf_op jit(solution)/shard_map/returns/pallas_call | solution.py:534
  68.0 0.6 copy.11
  68.6 0.6 copy.12
Async XLA Ops:
  0.6 26.2 %copy-start = (s32[512]{0:T(512)S(1)}, s32[512]{0:T(512)}, u32[]{:S(2)}) copy-start(s32[512]{0:T(512)} %len_ref.1) | copy-start | bytes 6148
  0.6 26.2 %copy-start.1 = (f32[4,128]{1,0:T(4,128)S(1)}, f32[4,128]{1,0:T(4,128)}, u32[]{:S(2)}) copy-start(f32[4,128]{1,0:T(4,128)} %lev_ref.1) | copy-start | bytes 6148

commit v3 on v2

--- a/solution.py
+++ b/solution.py
@@ -16,7 +16,7 @@
 UNITS = 8
 BATCH = 32
 PIECE = 1024
-OPENING = 16
+OPENING = 8
 
 
 def greet(axis_peers):
@@ -28,7 +28,7 @@
                 barrier, inc=1, device_id={axis: lax.rem(me + d, size)}, device_id_type=MESH
             )
             total += 1
-    pl.semaphore_wait(barrier, total)
+    return lambda: pl.semaphore_wait(barrier, total)
 
 
 def push(src, dst, send, recv, axis, peer):
@@ -74,16 +74,26 @@
         )
         for b in range(later)
     ]
+    codes_copy = pltpu.make_async_copy(codes_hbm, codes_ref, codes_sem)
+    words_copy = pltpu.make_async_copy(words_hbm, words_ref, wsem)
+    cand_copy.wait()
+    row_buf[me_c] = jnp.concatenate([cand_ref[0:1, :], cand_ref[1:2, :]], axis=1)
+    greeted = greet((("cent", me_c, cents), ("grp", me_g, groups)))
+    own.wait()
     fetch[0].start()
-    codes_copy = pltpu.make_async_copy(codes_hbm, codes_ref, codes_sem)
     codes_copy.start()
     for copy in fetch[1:] + fetch_tail:
         copy.start()
-    words_copy = pltpu.make_async_copy(words_hbm, words_ref, wsem)
     words_copy.start()
-    cand_copy.wait()
-    row_buf[me_c] = jnp.concatenate([cand_ref[0:1, :], cand_ref[1:2, :]], axis=1)
-    greet((("cent", me_c, cents), ("grp", me_g, groups)))
+    for t in range(tiles):
+        qt_ref[t] = qall_ref[me_g, t * width : (t + 1) * width, :].T
+    acc_ref[...] = jnp.full(acc_ref.shape, -jnp.inf, jnp.float32)
+    codes_copy.wait()
+    by_token = codes_ref[...].T
+    for part in range(codes_ref.shape[1] // 32):
+        span = slice(part * pass_dev, (part + 1) * pass_dev)
+        picks_ref[:, span] = by_token[part * 32 : (part + 1) * 32, :]
+    greeted()
 
     gather_rows = [
         push(row_buf.at[me_c], row_buf.at[me_c], s1.at[d], r1.at[d], "cent", lax.rem(me_c + d, cents))
@@ -115,18 +125,8 @@
 
     for copy in gather_rows:
         copy.start()
-    own.wait()
     for copy in (ahead_low, behind_high, ahead_high, behind_low, to_partner):
         copy.start()
-
-    for t in range(tiles):
-        qt_ref[t] = qall_ref[me_g, t * width : (t + 1) * width, :].T
-    acc_ref[...] = jnp.full(acc_ref.shape, -jnp.inf, jnp.float32)
-    codes_copy.wait()
-    by_token = codes_ref[...].T
-    for part in range(codes_ref.shape[1] // 32):
-        span = slice(part * pass_dev, (part + 1) * pass_dev)
-        picks_ref[:, span] = by_token[part * 32 : (part + 1) * 32, :]
 
     def step(b, _):
         here = pl.ds(pl.multiple_of(b * block, block), block)
@@ -217,7 +217,7 @@
     cents, groups, pass_dev, plen, qtok, opening,
     entries, len_ref, ends_ref, lev_ref, picks_ref, table, tail, words, q_ref, qt_ref, acc_in,
     out_ref, best_ref,
-    items, starts, units, seen, embeds, totals, acc, spread, csem, *picks,
+    items, starts, units, seen, dense, embeds, totals, acc, spread, csem, *picks,
 ):
     srcs = groups * cents
     tiles = qt_ref.shape[0]
@@ -270,6 +270,7 @@
         seen[k] = -1
         return 0
 
+    seen[pass_dev] = 0
     lax.fori_loop(0, pass_dev, forget, 0, unroll=16)
     count, used = lax.fori_loop(0, opening, open_step, (jnp.int32(0), jnp.int32(0)))
     for pad in range(BATCH):
@@ -300,15 +301,24 @@
             residual = jnp.where(
                 high, jnp.where(low, level[3], level[2]), jnp.where(low, level[1], level[0])
             )
-            dense = rows + residual
-            squares = jnp.sum(dense * dense, axis=1, keepdims=True)
-            tiles.append(dense * lax.rsqrt(squares + 1e-06))
-        return jnp.concatenate(tiles, axis=0).astype(jnp.bfloat16)
+            tiles.append(rows + residual)
+        return tiles
+
+    def finish(turn):
+        for k in range(UNITS):
+            tiles = []
+            for j in range(4):
+                value = dense[k * 32 + j * 8 : k * 32 + j * 8 + 8, :]
+                squares = jnp.sum(value * value, axis=1, keepdims=True)
+                tiles.append(value * lax.rsqrt(squares + 1e-06))
+            at = pl.multiple_of(turn * (UNITS * 32) + k * 32, 32)
+            embeds[pl.ds(at, 32), :] = jnp.concatenate(tiles, axis=0).astype(jnp.bfloat16)
 
     def embed_step(i, _):
-        values = [embed(units[i * UNITS + k]) for k in range(UNITS)]
-        for k, value in enumerate(values):
-            embeds[pl.ds(pl.multiple_of(i * (UNITS * 32) + k * 32, 32), 32), :] = value
+        finish(i)
+        for k in range(UNITS):
+            for j, tile in enumerate(embed(units[i * UNITS + k])):
+                dense[k * 32 + j * 8 : k * 32 + j * 8 + 8, :] = tile
         return 0
 
     def piece_step(m, _):
@@ -324,7 +334,8 @@
     lax.fori_loop(0, shared, both_step, 0)
     lax.fori_loop(shared, turns, embed_step, 0)
     lax.fori_loop(opening + shared, pieces, piece_step, 0)
-    embeds[pl.ds(pl.multiple_of(turns * (UNITS * 32), 32), plen), :] = jnp.zeros(
+    finish(turns)
+    embeds[pl.ds(pl.multiple_of((turns + 1) * (UNITS * 32), 32), plen), :] = jnp.zeros(
         (plen, embeds.shape[1]), embeds.dtype
     )
     for t in range(tiles):
@@ -345,7 +356,7 @@
                 length = len_ref[jnp.bitwise_and(entry, pass_dev - 1)]
                 wide[n * qtok : (n + 1) * qtok, n * 128 : (n + 1) * 128] = q_ref[query]
                 limit = length if limit is None else jnp.where(lane_q >= n * qtok, length, limit)
-                held.append(embeds[pl.ds(pl.multiple_of(starts[i] * 32, 32), plen), :])
+                held.append(embeds[pl.ds(pl.multiple_of((starts[i] + UNITS) * 32, 32), plen), :])
             scores = lax.dot_general(
                 jnp.concatenate(held, axis=1), wide[...], (((1,), (1,)), ((), ())), preferred_element_type=jnp.float32
             )
@@ -382,7 +393,7 @@
     best_buf, part_buf, sum_buf, row_buf, sb, rb, s1, r1, s2, r2,
 ):
     me_c, me_g = lax.axis_index("cent"), lax.axis_index("grp")
-    greet((("cent", me_c, cents), ("grp", me_g, groups)))
+    greet((("cent", me_c, cents), ("grp", me_g, groups)))()
 
     def rows_of(g):
         return part_ref.at[pl.ds(pl.multiple_of(g * cents, cents), cents)]
@@ -508,7 +519,8 @@
             pltpu.SMEM((slots + BATCH,), i32),
             pltpu.SMEM((slots * (plen // 32) + UNITS + 4,), i32),
             pltpu.SMEM((pass_dev + 1,), i32),
-            pltpu.VMEM((slots * plen + UNITS * 32 + plen, width), bf16),
+            pltpu.VMEM((UNITS * 32, width), f32),
+            pltpu.VMEM((slots * plen + 2 * UNITS * 32 + plen, width), bf16),
             pltpu.VMEM((slots + 8, 128), f32),
             pltpu.VMEM((tiles, 8, 256), f32),
             [pltpu.VMEM((128, 128 // qtok * width), bf16) for _ in range(BATCH * qtok // 128)],

time: 69.6 us -> 66.6 us (0.957)
  Pallas kernels: 67.3 us -> 64.4 us
    pallas_call x1, Pallas kernels: 26.1 us -> 24 us  [shards(): pl.pallas_call(functools.partial(search_kernel, cents, groups, pass_dev,...]
    pallas_call x1, Pallas kernels: 15.8 us -> 15 us  [shards(): pl.pallas_call(functools.partial(return_kernel, cents, groups), out_shape...]
where the time goes in v3:
time: 66.6 us; the launch traced here: 66.3 us
  Pallas kernels  64.4 us (97%)
  local copies, waits for them, and re-layouts  1.18 us (2%)
  between operations  0.69 us (1%)
    pallas_call x1, Pallas kernels, shards(): pl.pallas_call(functools.partial(passage_kernel, cents, groups, pass_dev,...  25.5 us
    pallas_call x1, Pallas kernels, shards(): pl.pallas_call(functools.partial(search_kernel, cents, groups, pass_dev,...  24 us
    pallas_call x1, Pallas kernels, shards(): pl.pallas_call(functools.partial(return_kernel, cents, groups), out_shape...  15 us

profile of v3, /device:TPU:0, one launch (start us, length us, event | category | flops | bytes accessed | tf_op | source)
XLA Modules:
  0.0 66.3 jit_solution(15870878257124267726)
XLA Ops:
  0.6 0.0 copy-start
  0.6 0.0 copy-start.1
  0.7 24.0 %search.1 = (f32[32768,128]{1,0:T(8,128)S(1)}, bf16[16384,128]{1,0:T(8,128)(2,1)S(1)}, s32[512,32,128]{2,1,0:T(8,128)S(1)}, bf16[8,1024,128]{2,1,0:T(8,128)(2,1)...) custom-call(bf16[1024,128]{1,0:T(8,128)(2,1)} %bitcast.8, ...), custom_call_target="tpu_custom_call" | custom-call | tf_op jit(solution)/shard_map/search/pallas_call | solution.py:464
  24.6 0.0 copy-done
  24.6 0.0 copy-done.1
  24.6 25.5 %passages.1 = (f32[128,128]{1,0:T(8,128)S(1)}, f32[1,1024]{1,0:T(1,128)S(1)}) custom-call(s32[1024]{0:T(1024)S(1)} %bitcast.6, s32[512]{0:T(512)S(1)} %copy-done, f32[128,128]{1,0:T(8,128)S(1)} %get-tuple-element.16.ends_ref, f32[4,128]{1,0:T(4,128)S(1)} %copy-done.1, s32[32,2048]{1,0:T(8,128)S(1)} %get-tuple-element.17.picks_ref, ...), custom_call_target="tpu_custom_call" | custom-call | tf_op jit(solution)/shard_map/passages/pallas_call | solution.py:512
  50.2 15.0 %returns.1 = (f32[32,32]{1,0:T(8,128)S(1)}, f32[2,64]{1,0:T(2,128)S(1)}) custom-call(f32[1,1024]{1,0:T(1,128)S(1)} %get-tuple-element.24.best_ref, f32[128,128]{1,0:T(8,128)S(1)} %get-tuple-element.25.part_ref), custom_call_target="tpu_custom_call" | custom-call | tf_op jit(solution)/shard_map/returns/pallas_call | solution.py:546
  65.1 0.6 copy.11
  65.7 0.6 copy.12
Async XLA Ops:
  0.6 24.0 %copy-start = (s32[512]{0:T(512)S(1)}, s32[512]{0:T(512)}, u32[]{:S(2)}) copy-start(s32[512]{0:T(512)} %len_ref.1) | copy-start | bytes 6148
  0.6 24.0 %copy-start.1 = (f32[4,128]{1,0:T(4,128)S(1)}, f32[4,128]{1,0:T(4,128)}, u32[]{:S(2)}) copy-start(f32[4,128]{1,0:T(4,128)} %lev_ref.1) | copy-start | bytes 6148

commit v4 on v3

--- a/solution.py
+++ b/solution.py
@@ -132,7 +132,7 @@
         here = pl.ds(pl.multiple_of(b * block, block), block)
         pltpu.make_async_copy(cent_hbm.at[here], head_buf.at[here], csem.at[b]).wait()
 
-        @pl.when(b == 2)
+        @pl.when(b == 4)
         def _():
             for copy in gather_rows:
                 copy.wait_recv()
@@ -148,13 +148,23 @@
             relay_behind.start()
             shares[1].start()
 
-        @pl.when(b == 6)
+        @pl.when(b == 5)
         def _():
             ahead_high.wait_recv()
             shares[2].start()
             behind_low.wait_recv()
             shares[3].start()
 
+        @pl.when(b == 7)
+        def _():
+            relay_ahead.wait_recv()
+            shares[4].start()
+            relay_behind.wait_recv()
+            shares[5].start()
+
+        beyond = pl.ds(pl.multiple_of(head + b * block, block), block)
+        pltpu.make_async_copy(cent_hbm.at[beyond], tail_ref.at[here], tsem.at[b]).wait()
+        table_ref[beyond, :] = tail_ref[here, :].astype(jnp.float32)
         table_ref[here, :] = head_buf[here, :].astype(jnp.float32)
         for t in range(tiles):
             scores = jnp.dot(head_buf[here, :], qt_ref[t], preferred_element_type=jnp.float32)
@@ -163,22 +173,6 @@
         return 0
 
     lax.fori_loop(0, steps, step, 0)
-    for copy in fetch_tail:
-        copy.wait()
-    part_rows = 1024
-
-    def widen(r, _):
-        src = pl.ds(pl.multiple_of(r * part_rows, part_rows), part_rows)
-        dst = pl.ds(pl.multiple_of(head + r * part_rows, part_rows), part_rows)
-        table_ref[dst, :] = tail_ref[src, :].astype(jnp.float32)
-        return 0
-
-    lax.fori_loop(0, tail_ref.shape[0] // part_rows, widen, 0)
-
-    relay_ahead.wait_recv()
-    shares[4].start()
-    relay_behind.wait_recv()
-    shares[5].start()
     for copy in gather_groups:
         copy.wait_recv()
     all_buf[me_g] = row_buf[...]

time: 66.6 us -> 63.8 us (0.958)
  Pallas kernels: 64.4 us -> 61.6 us
    pallas_call x1, Pallas kernels: 25.5 us -> 24 us  [shards(): pl.pallas_call(functools.partial(passage_kernel, cents, groups, pass_dev,...]
    pallas_call x1, Pallas kernels: 24 us -> 22.7 us  [shards(): pl.pallas_call(functools.partial(search_kernel, cents, groups, pass_dev,...]
where the time goes in v4:
time: 63.8 us; the launch traced here: 63.4 us
  Pallas kernels  61.6 us (97%)
  local copies, waits for them, and re-layouts  1.18 us (2%)
  between operations  0.69 us (1%)
    pallas_call x1, Pallas kernels, shards(): pl.pallas_call(functools.partial(passage_kernel, cents, groups, pass_dev,...  24 us
    pallas_call x1, Pallas kernels, shards(): pl.pallas_call(functools.partial(search_kernel, cents, groups, pass_dev,...  22.7 us
    pallas_call x1, Pallas kernels, shards(): pl.pallas_call(functools.partial(return_kernel, cents, groups), out_shape...  14.8 us

profile of v4, /device:TPU:0, one launch (start us, length us, event | category | flops | bytes accessed | tf_op | source)
XLA Modules:
  0.0 63.4 jit_solution(8457275257288530310)
XLA Ops:
  0.6 0.0 copy-start
  0.6 0.0 copy-start.1
  0.7 22.7 %search.1 = (f32[32768,128]{1,0:T(8,128)S(1)}, bf16[16384,128]{1,0:T(8,128)(2,1)S(1)}, s32[512,32,128]{2,1,0:T(8,128)S(1)}, bf16[8,1024,128]{2,1,0:T(8,128)(2,1)...) custom-call(bf16[1024,128]{1,0:T(8,128)(2,1)} %bitcast.8, ...), custom_call_target="tpu_custom_call" | custom-call | tf_op jit(solution)/shard_map/search/pallas_call | solution.py:458
  23.4 0.0 copy-done
  23.4 0.0 copy-done.1
  23.4 24.0 %passages.1 = (f32[128,128]{1,0:T(8,128)S(1)}, f32[1,1024]{1,0:T(1,128)S(1)}) custom-call(s32[1024]{0:T(1024)S(1)} %bitcast.6, s32[512]{0:T(512)S(1)} %copy-done, f32[128,128]{1,0:T(8,128)S(1)} %get-tuple-element.16.ends_ref, f32[4,128]{1,0:T(4,128)S(1)} %copy-done.1, s32[32,2048]{1,0:T(8,128)S(1)} %get-tuple-element.17.picks_ref, ...), custom_call_target="tpu_custom_call" | custom-call | tf_op jit(solution)/shard_map/passages/pallas_call | solution.py:506
  47.4 14.8 %returns.1 = (f32[32,32]{1,0:T(8,128)S(1)}, f32[2,64]{1,0:T(2,128)S(1)}) custom-call(f32[1,1024]{1,0:T(1,128)S(1)} %get-tuple-element.24.best_ref, f32[128,128]{1,0:T(8,128)S(1)} %get-tuple-element.25.part_ref), custom_call_target="tpu_custom_call" | custom-call | tf_op jit(solution)/shard_map/returns/pallas_call | solution.py:540
  62.2 0.6 copy.11
  62.9 0.6 copy.12
Async XLA Ops:
  0.6 22.7 %copy-start = (s32[512]{0:T(512)S(1)}, s32[512]{0:T(512)}, u32[]{:S(2)}) copy-start(s32[512]{0:T(512)} %len_ref.1) | copy-start | bytes 6148
  0.6 22.7 %copy-start.1 = (f32[4,128]{1,0:T(4,128)S(1)}, f32[4,128]{1,0:T(4,128)}, u32[]{:S(2)}) copy-start(f32[4,128]{1,0:T(4,128)} %lev_ref.1) | copy-start | bytes 6148

commit v5 on v4

--- a/solution.py
+++ b/solution.py
@@ -208,10 +208,10 @@
 
 
 def passage_kernel(
-    cents, groups, pass_dev, plen, qtok, opening,
-    entries, len_ref, ends_ref, lev_ref, picks_ref, table, tail, words, q_ref, qt_ref, acc_in,
-    out_ref, best_ref,
-    items, starts, units, seen, dense, embeds, totals, acc, spread, csem, *picks,
+    cents, groups, pass_dev, plen, opening,
+    entries, len_ref, lev_ref, picks_ref, table, tail, words, qt_ref, acc_in,
+    embeds, starts, best_ref,
+    units, seen, dense, acc, csem, *picks,
 ):
     srcs = groups * cents
     tiles = qt_ref.shape[0]
@@ -233,8 +233,7 @@
         top = jnp.max(scores.reshape(rows_of_piece // 8, 8, scores.shape[1]), axis=0)
         acc[t] = jnp.maximum(acc[t], top)
 
-    def collect(src, state):
-        count, used = state
+    def collect(src, used):
         pair = [entries[slot * srcs + src] for slot in range(2)]
         there = [entry >= 0 for entry in pair]
         owned = [jnp.bitwise_and(entry, pass_dev - 1) for entry in pair]
@@ -243,14 +242,12 @@
         sizes = [jnp.right_shift(len_ref[passage] + 31, 5) for passage in owned]
         for n in range(2):
             at = jnp.where(known[n] < 0, used, known[n])
-            items[count] = pair[n]
-            starts[count] = at
+            starts[n * srcs + src] = jnp.where(there[n], at, 0) + UNITS
             seen[marks[n]] = at
             for part in range(plen // 32):
                 units[used + part] = owned[n] + part * pass_dev
-            count = count + jnp.where(there[n], 1, 0)
             used = used + jnp.where(there[n] & (known[n] < 0), sizes[n], 0)
-        return count, used
+        return used
 
     def open_step(m, state):
         piece(m)
@@ -258,21 +255,15 @@
             state = collect(m * (srcs // opening) + k, state)
         return state
 
-    for k in range(len(spread)):
-        spread[k][...] = jnp.zeros(spread[k].shape, spread[k].dtype)
     def forget(k, _):
         seen[k] = -1
         return 0
 
     seen[pass_dev] = 0
     lax.fori_loop(0, pass_dev, forget, 0, unroll=16)
-    count, used = lax.fori_loop(0, opening, open_step, (jnp.int32(0), jnp.int32(0)))
-    for pad in range(BATCH):
-        items[count + pad] = 2 * srcs * (2 * srcs) * pass_dev
-        starts[count + pad] = 0
+    used = lax.fori_loop(0, opening, open_step, jnp.int32(0))
     for pad in range(UNITS):
         units[used + pad] = 0
-    totals[...] = jnp.zeros(totals.shape, jnp.float32)
     for copy in loads:
         copy.wait()
 
@@ -305,8 +296,7 @@
                 value = dense[k * 32 + j * 8 : k * 32 + j * 8 + 8, :]
                 squares = jnp.sum(value * value, axis=1, keepdims=True)
                 tiles.append(value * lax.rsqrt(squares + 1e-06))
-            at = pl.multiple_of(turn * (UNITS * 32) + k * 32, 32)
-            embeds[pl.ds(at, 32), :] = jnp.concatenate(tiles, axis=0).astype(jnp.bfloat16)
+            embeds[turn * UNITS + k] = jnp.concatenate(tiles, axis=0).astype(jnp.bfloat16)
 
     def embed_step(i, _):
         finish(i)
@@ -329,28 +319,43 @@
     lax.fori_loop(shared, turns, embed_step, 0)
     lax.fori_loop(opening + shared, pieces, piece_step, 0)
     finish(turns)
-    embeds[pl.ds(pl.multiple_of((turns + 1) * (UNITS * 32), 32), plen), :] = jnp.zeros(
-        (plen, embeds.shape[1]), embeds.dtype
-    )
+    for k in range(plen // 32):
+        embeds[(turns + 1) * UNITS + k] = jnp.zeros(embeds.shape[1:], embeds.dtype)
     for t in range(tiles):
         width = acc.shape[2]
         best_ref[:, t * width : (t + 1) * width] = jnp.max(acc[t], axis=0, keepdims=True)
 
+
+def return_kernel(
+    cents, groups, pass_dev, plen, qtok,
+    entries, len_ref, starts, ends_ref, embeds, q_ref, best_ref,
+    token_ref, score_ref,
+    part_ref, totals, spread, best_buf, part_buf, sum_buf, row_buf, sb, rb, s1, r1, s2, r2,
+):
+    me_c, me_g = lax.axis_index("cent"), lax.axis_index("grp")
+    srcs = cents * groups
+    greeted = greet((("cent", me_c, cents), ("grp", me_g, groups)))
     lane_q = lax.broadcasted_iota(jnp.int32, (8, 128), 1)
     four = 128 // qtok
 
+    sub = lax.broadcasted_iota(jnp.int32, (8, 128), 0)
+    for wide in spread:
+        wide[...] = jnp.zeros(wide.shape, wide.dtype)
+
     def score_step(batch, _):
         for k, wide in enumerate(spread):
-            limit, rows, held = None, [], []
+            limit, held = None, []
             for n in range(four):
                 i = batch * BATCH + k * four + n
-                entry = items[i]
+                entry = entries[i]
                 query = jnp.bitwise_and(jnp.right_shift(entry, pass_dev.bit_length() - 1), 2 * srcs - 1)
-                rows.append(jnp.right_shift(entry, (2 * srcs * pass_dev).bit_length() - 1))
                 length = len_ref[jnp.bitwise_and(entry, pass_dev - 1)]
                 wide[n * qtok : (n + 1) * qtok, n * 128 : (n + 1) * 128] = q_ref[query]
                 limit = length if limit is None else jnp.where(lane_q >= n * qtok, length, limit)
-                held.append(embeds[pl.ds(pl.multiple_of((starts[i] + UNITS) * 32, 32), plen), :])
+                first = starts[i]
+                held.append(
+                    jnp.concatenate([embeds[first + part] for part in range(plen // 32)], axis=0)
+                )
             scores = lax.dot_general(
                 jnp.concatenate(held, axis=1), wide[...], (((1,), (1,)), ((), ())), preferred_element_type=jnp.float32
             )
@@ -364,30 +369,21 @@
             line = jnp.max(top, axis=0, keepdims=True)
             for n in range(four):
                 own = (lane_q[0:1] >= n * qtok) & (lane_q[0:1] < (n + 1) * qtok)
-                totals[pl.ds(rows[n], 1), :] = jnp.where(own, line, 0.0)
+                totals[pl.ds(batch * BATCH + k * four + n, 1), :] = jnp.where(own, line, 0.0)
         return 0
 
-    lax.fori_loop(0, pl.cdiv(count, BATCH), score_step, 0)
-
-    value = jnp.sum(totals[0 : 2 * srcs, :], axis=1, keepdims=True) * (1.0 / qtok)
+    lax.fori_loop(0, 2 * srcs // BATCH, score_step, 0)
+
+    value = jnp.sum(totals[...], axis=1, keepdims=True) * (1.0 / qtok)
     ends = ends_ref[...]
     lane = lax.broadcasted_iota(jnp.int32, (srcs, srcs), 1)
     place = jnp.right_shift(ends.astype(jnp.int32), pass_dev.bit_length() - 1)
     low, high = place[:, 0:1], place[:, 1:2]
     second = ends[:, 1:2] > ends[:, 0:1]
-    out_ref[...] = jnp.where(lane == low, value[0:srcs], 0.0) + jnp.where(
+    part_ref[...] = jnp.where(lane == low, value[0:srcs], 0.0) + jnp.where(
         (lane == high) & second, value[srcs : 2 * srcs], 0.0
     )
-
-
-def return_kernel(
-    cents, groups,
-    best_ref, part_ref,
-    token_ref, score_ref,
-    best_buf, part_buf, sum_buf, row_buf, sb, rb, s1, r1, s2, r2,
-):
-    me_c, me_g = lax.axis_index("cent"), lax.axis_index("grp")
-    greet((("cent", me_c, cents), ("grp", me_g, groups)))()
+    greeted()
 
     def rows_of(g):
         return part_ref.at[pl.ds(pl.multiple_of(g * cents, cents), cents)]
@@ -491,7 +487,7 @@
             dma((13,)),
         ],
         compiler_params=pltpu.CompilerParams(
-            collective_id=0, has_side_effects=True, vmem_limit_bytes=8 * mib
+            collective_id=0, has_side_effects=True, vmem_limit_bytes=6 * mib
         ),
         name="search",
     )(
@@ -503,46 +499,33 @@
     )
 
     slots = 2 * srcs
-    parts, best = pl.pallas_call(
-        functools.partial(passage_kernel, cents, groups, pass_dev, plen, qtok, OPENING),
-        out_shape=(sds((srcs, srcs), f32), sds((1, tokens), f32)),
-        in_specs=[SMEM, SMEM, VMEM, VMEM, ANY, VMEM, VMEM, VMEM, VMEM, VMEM, VMEM],
-        out_specs=(VMEM, VMEM),
+    held = (slots + 1) * (plen // 32) + 2 * UNITS
+    embeds, starts, best = pl.pallas_call(
+        functools.partial(passage_kernel, cents, groups, pass_dev, plen, OPENING),
+        out_shape=(sds((held, 32, width), bf16), sds((slots,), i32), sds((1, tokens), f32)),
+        in_specs=[SMEM, SMEM] + [VMEM, ANY] + [VMEM] * 5,
+        out_specs=(VMEM, SMEM, VMEM),
         scratch_shapes=[
-            pltpu.SMEM((slots + BATCH,), i32),
-            pltpu.SMEM((slots + BATCH,), i32),
             pltpu.SMEM((slots * (plen // 32) + UNITS + 4,), i32),
             pltpu.SMEM((pass_dev + 1,), i32),
             pltpu.VMEM((UNITS * 32, width), f32),
-            pltpu.VMEM((slots * plen + 2 * UNITS * 32 + plen, width), bf16),
-            pltpu.VMEM((slots + 8, 128), f32),
             pltpu.VMEM((tiles, 8, 256), f32),
-            [pltpu.VMEM((128, 128 // qtok * width), bf16) for _ in range(BATCH * qtok // 128)],
             dma((32,)),
             *[pltpu.SMEM((plen // 32 * pass_dev,), i32) for _ in range(32)],
         ],
-        compiler_params=pltpu.CompilerParams(vmem_limit_bytes=14 * mib),
+        compiler_params=pltpu.CompilerParams(vmem_limit_bytes=2 * mib),
         name="passages",
-    )(
-        entries.reshape(8 * srcs),
-        lengths,
-        ends,
-        levels,
-        picks,
-        table,
-        tail,
-        words,
-        qall.reshape(groups * query_rows, qtok, width),
-        qt,
-        acc,
-    )
+    )(entries.reshape(8 * srcs), lengths, levels, picks, table, tail, words, qt, acc)
 
     token_best, scores = pl.pallas_call(
-        functools.partial(return_kernel, cents, groups),
+        functools.partial(return_kernel, cents, groups, pass_dev, plen, qtok),
         out_shape=(sds((query_rows, qtok), f32), sds((per_device, cand_count), f32)),
-        in_specs=[VMEM, VMEM],
+        in_specs=[SMEM] * 3 + [VMEM] * 4,
         out_specs=(VMEM, VMEM),
         scratch_shapes=[
+            pltpu.VMEM((srcs, srcs), f32),
+            pltpu.VMEM((slots, 128), f32),
+            [pltpu.VMEM((128, 128 // qtok * width), bf16) for _ in range(BATCH * qtok // 128)],
             pltpu.VMEM((cents, 1, tokens), f32),
             pltpu.VMEM((groups, cents, srcs), f32),
             pltpu.VMEM((cents, 1, srcs), f32),
@@ -558,7 +541,15 @@
             collective_id=1, has_side_effects=True, vmem_limit_bytes=4 * mib
         ),
         name="returns",
-    )(best, parts)
+    )(
+        entries.reshape(8 * srcs),
+        lengths,
+        starts,
+        ends,
+        embeds,
+        qall.reshape(groups * query_rows, qtok, width),
+        best,
+    )
     return token_best, scores.reshape(1, 1, per_device, cand_count)
 
 

time: 63.8 us -> 63.2 us (level)
  no operation moved by 1% of the time
where the time goes in v5:
time: 63.2 us; the launch traced here: 62.8 us
  Pallas kernels  61 us (97%)
  local copies, waits for them, and re-layouts  1.18 us (2%)
  between operations  0.69 us (1%)
    pallas_call x1, Pallas kernels, shards(): pl.pallas_call(functools.partial(passage_kernel, cents, groups, pass_dev,...  23.4 us
    pallas_call x1, Pallas kernels, shards(): pl.pallas_call(functools.partial(search_kernel, cents, groups, pass_dev,...  22.7 us
    pallas_call x1, Pallas kernels, shards(): pl.pallas_call(functools.partial(return_kernel, cents, groups, pass_dev,...  14.8 us

profile of v5, /device:TPU:0, one launch (start us, length us, event | category | flops | bytes accessed | tf_op | source)
XLA Modules:
  0.0 62.8 jit_solution(16739512185371577712)
XLA Ops:
  0.6 0.0 copy-start
  0.6 0.0 copy-start.1
  0.7 22.7 %search.1 = (f32[32768,128]{1,0:T(8,128)S(1)}, bf16[16384,128]{1,0:T(8,128)(2,1)S(1)}, s32[512,32,128]{2,1,0:T(8,128)S(1)}, bf16[8,1024,128]{2,1,0:T(8,128)(2,1)...) custom-call(bf16[1024,128]{1,0:T(8,128)(2,1)} %bitcast.9, ...), custom_call_target="tpu_custom_call" | custom-call | tf_op jit(solution)/shard_map/search/pallas_call | solution.py:454
  23.4 0.0 copy-done
  23.4 0.0 copy-done.1
  23.4 23.4 %passages.1 = (bf16[1044,32,128]{2,1,0:T(8,128)(2,1)S(1)}, s32[256]{0:T(256)S(1)}, f32[1,1024]{1,0:T(1,128)S(1)}) custom-call(s32[1024]{0:T(1024)S(1)} %bitcast.6, s32[512]{0:T(512)S(1)} %copy-done, f32[4,128]{1,0:T(4,128)S(1)} %copy-done.1, s32[32,2048]{1,0:T(8,128)S(1)} %get-tuple-element.17.picks_ref, f32[32768,128]{1,0:T(8,128)S(1)} %get-tuple-element.18.table, ...), custom_call_target="tpu_custom_call" | custom-call | tf_op jit(solution)/shard_map/passages/pallas_call | solution.py:503
  46.8 14.8 %returns.1 = (f32[32,32]{1,0:T(8,128)S(1)}, f32[2,64]{1,0:T(2,128)S(1)}) custom-call(s32[1024]{0:T(1024)S(1)} %bitcast.7, s32[512]{0:T(512)S(1)} %copy-done, s32[256]{0:T(256)S(1)} %get-tuple-element.23.starts, f32[128,128]{1,0:T(8,128)S(1)} %get-tuple-element.24.ends_ref, bf16[1044,32,128]{2,1,0:T(8,128)(2,1)S(1)} %get-tuple-element.25.embeds, ...), custom_call_target="tpu_custom_call" | custom-call | tf_op jit(solution)/shard_map/returns/pallas_call | solution.py:520
  61.7 0.6 copy.11
  62.3 0.6 copy.12
Async XLA Ops:
  0.6 22.7 %copy-start = (s32[512]{0:T(512)S(1)}, s32[512]{0:T(512)}, u32[]{:S(2)}) copy-start(s32[512]{0:T(512)} %len_ref.3) | copy-start | bytes 6148
  0.6 22.7 %copy-start.1 = (f32[4,128]{1,0:T(4,128)S(1)}, f32[4,128]{1,0:T(4,128)}, u32[]{:S(2)}) copy-start(f32[4,128]{1,0:T(4,128)} %lev_ref.1) | copy-start | bytes 6148

commit v6 on v5

--- a/solution.py
+++ b/solution.py
@@ -15,7 +15,7 @@
 MASKED = -1000000000.0
 UNITS = 8
 BATCH = 32
-PIECE = 1024
+PIECE = 2048
 OPENING = 8
 
 

time: 63.2 us -> 62.2 us (0.984)
  Pallas kernels: 61 us -> 60 us
    pallas_call x1, Pallas kernels: 23.4 us -> 17.4 us  [shards(): pl.pallas_call(functools.partial(passage_kernel, cents, groups, pass_dev,...]
    pallas_call x1, Pallas kernels: 14.8 us -> 20 us  [shards(): pl.pallas_call(functools.partial(return_kernel, cents, groups, pass_dev,...]
where the time goes in v6:
time: 62.2 us; the launch traced here: 61.9 us
  Pallas kernels  60 us (96%)
  local copies, waits for them, and re-layouts  1.18 us (2%)
  between operations  0.69 us (1%)
    pallas_call x1, Pallas kernels, shards(): pl.pallas_call(functools.partial(search_kernel, cents, groups, pass_dev,...  22.7 us
    pallas_call x1, Pallas kernels, shards(): pl.pallas_call(functools.partial(return_kernel, cents, groups, pass_dev,...  20 us
    pallas_call x1, Pallas kernels, shards(): pl.pallas_call(functools.partial(passage_kernel, cents, groups, pass_dev,...  17.4 us

profile of v6, /device:TPU:0, one launch (start us, length us, event | category | flops | bytes accessed | tf_op | source)
XLA Modules:
  0.0 61.9 jit_solution(8862144810824293300)
XLA Ops:
  0.6 0.0 copy-start
  0.6 0.0 copy-start.1
  0.7 22.7 %search.1 = (f32[32768,128]{1,0:T(8,128)S(1)}, bf16[16384,128]{1,0:T(8,128)(2,1)S(1)}, s32[512,32,128]{2,1,0:T(8,128)S(1)}, bf16[8,1024,128]{2,1,0:T(8,128)(2,1)...) custom-call(bf16[1024,128]{1,0:T(8,128)(2,1)} %bitcast.9, ...), custom_call_target="tpu_custom_call" | custom-call | tf_op jit(solution)/shard_map/search/pallas_call | solution.py:454
  23.4 0.0 copy-done
  23.4 0.0 copy-done.1
  23.4 17.4 %passages.1 = (bf16[1044,32,128]{2,1,0:T(8,128)(2,1)S(1)}, s32[256]{0:T(256)S(1)}, f32[1,1024]{1,0:T(1,128)S(1)}) custom-call(s32[1024]{0:T(1024)S(1)} %bitcast.6, s32[512]{0:T(512)S(1)} %copy-done, f32[4,128]{1,0:T(4,128)S(1)} %copy-done.1, s32[32,2048]{1,0:T(8,128)S(1)} %get-tuple-element.17.picks_ref, f32[32768,128]{1,0:T(8,128)S(1)} %get-tuple-element.18.table, ...), custom_call_target="tpu_custom_call" | custom-call | tf_op jit(solution)/shard_map/passages/pallas_call | solution.py:503
  40.8 20.0 %returns.1 = (f32[32,32]{1,0:T(8,128)S(1)}, f32[2,64]{1,0:T(2,128)S(1)}) custom-call(s32[1024]{0:T(1024)S(1)} %bitcast.7, s32[512]{0:T(512)S(1)} %copy-done, s32[256]{0:T(256)S(1)} %get-tuple-element.23.starts, f32[128,128]{1,0:T(8,128)S(1)} %get-tuple-element.24.ends_ref, bf16[1044,32,128]{2,1,0:T(8,128)(2,1)S(1)} %get-tuple-element.25.embeds, ...), custom_call_target="tpu_custom_call" | custom-call | tf_op jit(solution)/shard_map/returns/pallas_call | solution.py:520
  60.7 0.6 copy.11
  61.3 0.6 copy.12
Async XLA Ops:
  0.6 22.7 %copy-start = (s32[512]{0:T(512)S(1)}, s32[512]{0:T(512)}, u32[]{:S(2)}) copy-start(s32[512]{0:T(512)} %len_ref.3) | copy-start | bytes 6148
  0.6 22.7 %copy-start.1 = (f32[4,128]{1,0:T(4,128)S(1)}, f32[4,128]{1,0:T(4,128)}, u32[]{:S(2)}) copy-start(f32[4,128]{1,0:T(4,128)} %lev_ref.1) | copy-start | bytes 6148

commit v7 on v6

--- a/solution.py
+++ b/solution.py
@@ -13,8 +13,8 @@
 SMEM = pl.BlockSpec(memory_space=pltpu.SMEM)
 EMPTY = 1 << 20
 MASKED = -1000000000.0
-UNITS = 8
-BATCH = 32
+UNITS = 16
+BATCH = 64
 PIECE = 2048
 OPENING = 8
 

time: 62.2 us -> 61.4 us (0.987)
  Pallas kernels: 60 us -> 59 us
    pallas_call x1, Pallas kernels: 20 us -> 14.7 us  [shards(): pl.pallas_call(functools.partial(return_kernel, cents, groups, pass_dev,...]
    pallas_call x1, Pallas kernels: 17.4 us -> 21.6 us  [shards(): pl.pallas_call(functools.partial(passage_kernel, cents, groups, pass_dev,...]
where the time goes in v7:
time: 61.4 us; the launch traced here: 60.9 us
  Pallas kernels  59 us (96%)
  local copies, waits for them, and re-layouts  1.18 us (2%)
  between operations  0.69 us (1%)
    pallas_call x1, Pallas kernels, shards(): pl.pallas_call(functools.partial(search_kernel, cents, groups, pass_dev,...  22.7 us
    pallas_call x1, Pallas kernels, shards(): pl.pallas_call(functools.partial(passage_kernel, cents, groups, pass_dev,...  21.6 us
    pallas_call x1, Pallas kernels, shards(): pl.pallas_call(functools.partial(return_kernel, cents, groups, pass_dev,...  14.7 us

profile of v7, /device:TPU:0, one launch (start us, length us, event | category | flops | bytes accessed | tf_op | source)
XLA Modules:
  0.0 60.9 jit_solution(6508444311047858169)
XLA Ops:
  0.6 0.0 copy-start
  0.6 0.0 copy-start.1
  0.7 22.7 %search.1 = (f32[32768,128]{1,0:T(8,128)S(1)}, bf16[16384,128]{1,0:T(8,128)(2,1)S(1)}, s32[512,32,128]{2,1,0:T(8,128)S(1)}, bf16[8,1024,128]{2,1,0:T(8,128)(2,1)...) custom-call(bf16[1024,128]{1,0:T(8,128)(2,1)} %bitcast.9, ...), custom_call_target="tpu_custom_call" | custom-call | tf_op jit(solution)/shard_map/search/pallas_call | solution.py:454
  23.4 0.0 copy-done
  23.4 0.0 copy-done.1
  23.4 21.6 %passages.1 = (bf16[1060,32,128]{2,1,0:T(8,128)(2,1)S(1)}, s32[256]{0:T(256)S(1)}, f32[1,1024]{1,0:T(1,128)S(1)}) custom-call(s32[1024]{0:T(1024)S(1)} %bitcast.6, s32[512]{0:T(512)S(1)} %copy-done, f32[4,128]{1,0:T(4,128)S(1)} %copy-done.1, s32[32,2048]{1,0:T(8,128)S(1)} %get-tuple-element.17.picks_ref, f32[32768,128]{1,0:T(8,128)S(1)} %get-tuple-element.18.table, ...), custom_call_target="tpu_custom_call" | custom-call | tf_op jit(solution)/shard_map/passages/pallas_call | solution.py:503
  45.0 14.7 %returns.1 = (f32[32,32]{1,0:T(8,128)S(1)}, f32[2,64]{1,0:T(2,128)S(1)}) custom-call(s32[1024]{0:T(1024)S(1)} %bitcast.7, s32[512]{0:T(512)S(1)} %copy-done, s32[256]{0:T(256)S(1)} %get-tuple-element.23.starts, f32[128,128]{1,0:T(8,128)S(1)} %get-tuple-element.24.ends_ref, bf16[1060,32,128]{2,1,0:T(8,128)(2,1)S(1)} %get-tuple-element.25.embeds, ...), custom_call_target="tpu_custom_call" | custom-call | tf_op jit(solution)/shard_map/returns/pallas_call | solution.py:520
  59.7 0.6 copy.11
  60.3 0.6 copy.12
Async XLA Ops:
  0.6 22.7 %copy-start = (s32[512]{0:T(512)S(1)}, s32[512]{0:T(512)}, u32[]{:S(2)}) copy-start(s32[512]{0:T(512)} %len_ref.3) | copy-start | bytes 6148
  0.6 22.7 %copy-start.1 = (f32[4,128]{1,0:T(4,128)S(1)}, f32[4,128]{1,0:T(4,128)}, u32[]{:S(2)}) copy-start(f32[4,128]{1,0:T(4,128)} %lev_ref.1) | copy-start | bytes 6148
